TPU v7x, 32 devices: a whole 2x2x4 slice. The times are simulated.
32 devices in a mesh: groups: 1, expert: 8 (over z, core), dp: 4 (over y, x).
Axes of the slice: x: 2, y: 2, z: 4, core: 2. Of those that a mesh axis runs over, the one named last changes fastest.
Arguments:
- tokens: bfloat16 [128, 4096], P(('groups', 'expert', 'dp')), may hold values from -6 to 6
- expert_ids: int32 [128, 2], P(('groups', 'expert', 'dp')), may hold values from 0 to 7, as said below
- gate_weights: bfloat16 [128, 2], P(('groups', 'expert', 'dp')), may hold values from 0.099609375 to 1
- placement: int32 [2, 2], P('groups'), may hold values from 0 to 7, as said below
- w_gate: bfloat16 [8, 1536, 4096], P('expert', 'dp'), may hold values from -0.09375 to 0.09375
- w_up: bfloat16 [8, 1536, 4096], P('expert', 'dp'), may hold values from -0.09375 to 0.09375
- w_down: bfloat16 [8, 1536, 4096], P('expert', 'dp'), may hold values from -0.15625 to 0.15625
Outputs:
- mixed: bfloat16 [128, 4096], P(('groups', 'expert', 'dp'))
Inputs may be any that keep to these rules, and one draw needn't show every extreme that they name: `expert_ids`: each row names 2 different experts. In each aligned block of 16 rows (the tokens of one index of expert) no expert is named by more than 6 rows, and some expert is named by exactly that many. `placement`: row 0 holds 2 different experts; row 1 holds 2 different expert indices, none of which appears in row 0.
All inputs are finite; a program needn't handle non-finite values.
Results may differ from a plain program's by a relative error of at most 0.015.
Values may be sent and summed in bfloat16 or wider, within the bound.
No kernel may reach another device: no remote copies, remote signals or barrier semaphores. Data moves between devices by JAX's collectives and lax.ppermute only.
A program may use at most 64 MiB of HBM per device.

v0:
```python
import functools

import jax
import jax.numpy as jnp
from jax import lax
from jax.experimental import pallas as pl
from jax.experimental.pallas import tpu as pltpu
from jax.sharding import PartitionSpec as P


BF16, F32, I32 = jnp.bfloat16, jnp.float32, jnp.int32
CHUNKS = 8
LANES = 128


def iota(shape, dim):
    return lax.broadcasted_iota(I32, shape, dim)


def onehot(cond):
    return jnp.where(cond, 1.0, 0.0).astype(BF16)


def mm(a, b, contract=((1,), (0,))):
    return lax.dot_general(a, b, (contract, ((), ())), preferred_element_type=F32)


def dot(a, b, contract=((1,), (0,))):
    return mm(a.astype(BF16), b.astype(BF16), contract)


def partner(me, step, n):
    if n & (n - 1) == 0:
        return me ^ step
    return (step + n - me) % n


def swap(xs, axis):
    n = len(xs)
    out = [xs[0]]
    for j in range(1, n):
        out.append(lax.ppermute(xs[j], axis, [(i, partner(i, j, n)) for i in range(n)]))
    return out


def pack_kernel(tok_hbm, ids_hbm, gate_hbm, place_hbm, *refs):
    out_ref, spread_ref, earlier_ref, tok_ref, ids_ref, gate_ref, place_ref, sems = refs
    pairs = ((ids_hbm, ids_ref), (gate_hbm, gate_ref), (place_hbm, place_ref), (tok_hbm, tok_ref))
    copies = [pltpu.make_async_copy(a, b, sems.at[i]) for i, (a, b) in enumerate(pairs)]
    for copy in copies:
        copy.start()
    count, width = tok_ref.shape
    topk = ids_ref.shape[0]
    lanes = width // CHUNKS
    rows = count * CHUNKS
    extra = out_ref.shape[0] - rows
    me = lax.axis_index("dp")
    columns = spread_ref.shape[1]
    at = iota((LANES, columns), 1)
    token = partner(me, at // rows, columns // rows) * count + at % count
    spread_ref[...] = onehot(iota((LANES, columns), 0) == token)
    earlier_ref[...] = onehot(iota((LANES, columns), 0) < token)
    place = onehot(iota((count, LANES), 1) == iota((count, LANES), 0) + me * count)
    ids_row = onehot(iota((extra, topk), 0) == iota((extra, topk), 1))
    gate_row = onehot(iota((extra, topk), 0) == iota((extra, topk), 1) + topk)
    out_ref[rows:, 2 * LANES:] = jnp.zeros((extra, lanes - 2 * LANES), BF16)
    for copy in copies:
        copy.wait()
    for c in range(CHUNKS):
        out_ref[c * count:(c + 1) * count, :] = tok_ref[:, c * lanes:(c + 1) * lanes]
    small = dot(ids_row, (ids_ref[...] + 1).astype(F32)) + dot(gate_row, gate_ref[...])
    out_ref[rows:, :LANES] = dot(small, place).astype(BF16)
    line = iota((extra, LANES), 0)
    listed = jnp.zeros((extra, LANES), F32)
    for h in range(place_ref.shape[1]):
        listed = jnp.where(line == h, (place_ref[0:1, h:h + 1] + 1).astype(F32), listed)
    out_ref[rows:, LANES:2 * LANES] = listed.astype(BF16)


def row_experts(total, columns, piece, n_expert):
    step = iota((total, columns), 0) // piece
    return step, partner(lax.axis_index("expert"), step, n_expert).astype(F32) + 1.0


def select_kernel(n_expert, n_dp, first, slots, topk, hot, *refs):
    blocks, spread_ref, earlier_ref = refs[:n_dp], refs[n_dp], refs[n_dp + 1]
    sends = refs[n_dp + 2:n_dp + 2 + n_expert]
    pick_ref, small_ref, group_ref = refs[n_dp + 2 + n_expert:]
    per = group_ref.shape[0] // n_dp
    count = per // CHUNKS
    piece = slots * CHUNKS
    total = n_expert * piece
    columns = n_dp * per
    small = None
    for j, ref in enumerate(blocks):
        group_ref[j * per:(j + 1) * per, :] = ref[:per, :]
        part = ref[per:, :LANES].astype(F32)
        small = part if small is None else small + part
    places = blocks[0][per:, LANES:2 * LANES].astype(F32)
    _, expert = row_experts(total, LANES, piece, n_expert)
    named = jnp.zeros((total, LANES), F32)
    for k in range(topk):
        named = jnp.where(small[k:k + 1, :] == expert, 1.0, named)
    rank = dot(named, earlier_ref[...])
    spread = dot(small, spread_ref[...])
    small_ref[...] = spread
    step, expert = row_experts(total, columns, piece, n_expert)
    row, col = iota((total, columns), 0), iota((total, columns), 1)
    slot = ((row - step * piece) // CHUNKS).astype(F32)
    allowed = slot < first
    for h in range(hot):
        allowed |= expert == places[h:h + 1, :1]
    hit = None
    for k in range(topk):
        same = spread[k:k + 1, :] == expert
        hit = same if hit is None else hit | same
    chunk = row % CHUNKS == (col % per) // count
    pick = onehot(hit & allowed & chunk & (rank == slot))
    pick_ref[...] = pick
    value = mm(pick, group_ref[...]).astype(BF16)
    for j, ref in enumerate(sends):
        ref[...] = value[j * piece:(j + 1) * piece, :]


def expert_kernel(steps, *refs):
    ins, outs = refs[:steps], refs[steps + 4:2 * steps + 4]
    gate_ref, up_ref, down_ref, order_ref = refs[steps:steps + 4]
    x_ref, y_ref = refs[2 * steps + 4:]
    total, lanes = y_ref.shape
    piece = total // steps
    count = total // CHUNKS
    nt = ((1,), (1,))
    for j, ref in enumerate(ins):
        y_ref[j * piece:(j + 1) * piece, :] = ref[...]
    x = mm(order_ref[...], y_ref[...]).astype(BF16)
    for c in range(CHUNKS):
        x_ref[:, c * lanes:(c + 1) * lanes] = x[c * count:(c + 1) * count, :]
    gate = mm(x_ref[...], gate_ref[...], nt)
    up = mm(x_ref[...], up_ref[...], nt)
    hidden = (gate / (1.0 + jnp.exp(-gate)) * up).astype(BF16)
    for c in range(CHUNKS):
        value = mm(hidden, down_ref[:, c * lanes:(c + 1) * lanes]).astype(BF16)
        y_ref[c * count:(c + 1) * count, :] = value
    y = mm(order_ref[...], y_ref[...], ((0,), (0,))).astype(BF16)
    for j, ref in enumerate(outs):
        ref[...] = y[j * piece:(j + 1) * piece, :]


def mix_kernel(steps, *refs):
    backs, mix_ref, out_refs, rows_ref = refs[:steps], refs[steps], refs[steps + 1:-1], refs[-1]
    piece = backs[0].shape[0]
    for j, ref in enumerate(backs):
        rows_ref[j * piece:(j + 1) * piece, :] = ref[...]
    value = mm(mix_ref[...], rows_ref[...], ((0,), (0,))).astype(BF16)
    per = out_refs[0].shape[0]
    for j, ref in enumerate(out_refs):
        ref[...] = value[j * per:(j + 1) * per, :]


def finish_kernel(*refs):
    out_ref = refs[-1]
    total = refs[0][...].astype(F32)
    for ref in refs[1:-1]:
        total += ref[...].astype(F32)
    total = total.astype(BF16)
    lanes = total.shape[1]
    count = out_ref.shape[0]
    for c in range(CHUNKS):
        out_ref[:, c * lanes:(c + 1) * lanes] = total[c * count:(c + 1) * count, :]


def call(kernel, out_shape, in_specs=None, scratch=(), limit=8 << 20, **kw):
    return pl.pallas_call(
        kernel,
        out_shape=out_shape,
        scratch_shapes=scratch,
        compiler_params=pltpu.CompilerParams(vmem_limit_bytes=limit),
        **({} if in_specs is None else {"in_specs": in_specs}),
        **kw,
    )


def in_hbm(x):
    return pltpu.with_memory_space_constraint(x, pltpu.HBM)


def fetch_kernel(n_expert, topk, *refs):
    ins, pick_ref, small_ref, outs, order_ref, mix_ref, sems = (
        refs[:3], refs[3], refs[4], refs[5:8], refs[8], refs[9], refs[10]
    )
    copies = [pltpu.make_async_copy(a, b, sems.at[i]) for i, (a, b) in enumerate(zip(ins, outs))]
    for copy in copies:
        copy.start()
    total, columns = pick_ref.shape
    count = total // CHUNKS
    row, col = iota((total, total), 0), iota((total, total), 1)
    order_ref[...] = onehot(col == (row % count) * CHUNKS + row // count)
    _, expert = row_experts(total, columns, total // n_expert, n_expert)
    gate = jnp.zeros((total, columns), F32)
    for k in range(topk):
        hit = small_ref[k:k + 1, :] == expert
        gate = jnp.where(hit, small_ref[topk + k:topk + k + 1, :], gate)
    mix_ref[...] = jnp.where(pick_ref[...].astype(F32) > 0.0, gate, 0.0).astype(BF16)
    for copy in copies:
        copy.wait()


def body(tokens, expert_ids, gate_weights, placement, w_gate, w_up, w_down):
    n_expert, n_dp = lax.axis_size("expert"), lax.axis_size("dp")
    count, width = tokens.shape
    topk = expert_ids.shape[1]
    group = count * n_dp
    assert group <= LANES and n_expert < 256 and width % (CHUNKS * LANES) == 0
    assert width >= 2 * CHUNKS * LANES and placement.shape[1] <= 8
    first = max(2, group * topk // n_expert)
    slots = first + max(1, first // 2)
    lanes = width // CHUNKS
    per = count * CHUNKS
    extra = -(-2 * topk // 8) * 8
    total = n_expert * slots * CHUNKS
    shape = lambda *dims: jax.ShapeDtypeStruct(dims, BF16)
    hbm = pl.BlockSpec(memory_space=pltpu.HBM)
    big = total > 1024

    columns = n_dp * per
    table = shape(LANES, columns)
    packed, spread, earlier = call(
        pack_kernel,
        [shape(per + extra, lanes), table, table],
        [hbm] * 4,
        (
            pltpu.VMEM((count, width), BF16),
            pltpu.VMEM((topk, count), I32),
            pltpu.VMEM((topk, count), BF16),
            pltpu.VMEM(placement.shape, I32),
            pltpu.SemaphoreType.DMA((4,)),
        ),
    )(*map(in_hbm, (tokens, expert_ids.T, gate_weights.T, placement)))
    blocks = swap([packed] * n_dp, "dp")
    hot = placement.shape[1]
    *sends, pick, small = call(
        functools.partial(select_kernel, n_expert, n_dp, first, slots, topk, hot),
        [shape(slots * CHUNKS, lanes)] * n_expert
        + [shape(total, columns), jax.ShapeDtypeStruct((extra, columns), F32)],
        scratch=(pltpu.VMEM((columns, lanes), BF16),),
        limit=48 << 20 if big else 8 << 20,
    )(*blocks, spread, earlier)
    weights = [w[0] for w in (w_gate, w_up, w_down)]
    vmem = pl.BlockSpec(memory_space=pltpu.VMEM)
    *weights, order, mix = call(
        functools.partial(fetch_kernel, n_expert, topk),
        [shape(*w.shape) for w in weights] + [shape(total, total), shape(total, columns)],
        [hbm] * 3 + [vmem] * 2,
        (pltpu.SemaphoreType.DMA((3,)),),
        limit=48 << 20 if big else 16 << 20,
        cost_estimate=pl.CostEstimate(
            flops=0, bytes_accessed=sum(4 * w.size for w in weights), transcendentals=0
        ),
    )(*map(in_hbm, weights), pick, small)
    rows = swap(sends, "expert")
    parts = call(
        functools.partial(expert_kernel, n_expert),
        [shape(slots * CHUNKS, lanes)] * n_expert,
        scratch=(
            pltpu.VMEM((total // CHUNKS, width), BF16),
            pltpu.VMEM((total, lanes), BF16),
        ),
        limit=60 << 20 if big else 24 << 20,
    )(*rows, *weights, order)
    backs = swap(parts, "expert")
    outs = call(
        functools.partial(mix_kernel, n_expert),
        [shape(per, lanes)] * n_dp,
        scratch=(pltpu.VMEM((total, lanes), BF16),),
        limit=32 << 20 if big else 8 << 20,
    )(*backs, mix)
    pieces = swap(outs, "dp")
    return call(finish_kernel, shape(count, width))(*pieces)


def solution(mesh):
    placed = (
        P(("groups", "expert", "dp"), None),
        P(("groups", "expert", "dp"), None),
        P(("groups", "expert", "dp"), None),
        P("groups", None),
        P("expert", "dp", None),
        P("expert", "dp", None),
        P("expert", "dp", None),
    )
    return jax.shard_map(
        body,
        mesh=mesh,
        in_specs=placed,
        out_specs=P(("groups", "expert", "dp"), None),
        check_vma=False,
    )
```

profile of v0, /device:TPU:0, one launch (start us, length us, event | category | flops | bytes accessed | tf_op | source)
XLA Modules:
  0.0 47.0 jit_solution(18264698080185960486)
XLA Ops:
  0.0 1.1 %shard_map.73 = (bf16[40,512]{1,0:T(8,128)(2,1)S(1)}, bf16[128,128]{1,0:T(8,128)(2,1)S(1)}, bf16[128,128]{1,0:T(8,128)(2,1)S(1)}) custom-call(bf16[4,4096]{1,0:T(4,128)(2,1)} %tok_hbm.1, s32[2,4]{1,0:T(2,128)} %bitcast.8, bf16[2,4]{1,0:T(2,128)(2,1)} %bitcast.9, s32[2,2]{1,0:T(2,128)} %place_hbm.1), custom_call_target="tpu_custom_call" | custom-call | tf_op jit(solution)/shard_map/pallas_call | solution.py:227
  1.1 4.0 %collective-permute-start.2 = (bf16[40,512]{1,0:T(8,128)(2,1)S(1)}, bf16[40,512]{1,0:T(8,128)(2,1)S(1)}, u32[]{:S(2)}, u32[]{:S(2)}) collective-permute-start(bf16[40,512]{1,0:T(8,128)(2,1)S(1)} %get-tuple-element.35.refs_0_), channel_id=1, source_target_pairs={{0,3},{1,2},{2,1},{3,0},{4,7},{5,6},{6,5},{7,4},{8,11},{9,10},{10,... | collective-permute-start | bytes 122888 | tf_op jit(solution)/shard_map/ppermute | solution.py:42
  5.1 0.5 %collective-permute-start.1 = (bf16[40,512]{1,0:T(8,128)(2,1)S(1)}, bf16[40,512]{1,0:T(8,128)(2,1)S(1)}, u32[]{:S(2)}, u32[]{:S(2)}) collective-permute-start(bf16[40,512]{1,0:T(8,128)(2,1)S(1)} %get-tuple-element.35.refs_0_), channel_id=1, source_target_pairs={{0,2},{1,3},{2,0},{3,1},{4,6},{5,7},{6,4},{7,5},{8,10},{9,11},{10,... | collective-permute-start | bytes 122888 | tf_op jit(solution)/shard_map/ppermute | solution.py:42
  5.6 0.1 collective-permute-start
  5.7 1.3 %collective-permute-done.2.refs_3_ = bf16[40,512]{1,0:T(8,128)(2,1)S(1)} collective-permute-done((bf16[40,512]{1,0:T(8,128)(2,1)S(1)}, bf16[40,512]{1,0:T(8,128)(2,1)S(1)}, u32[]{:S(2)}, u32[]{:S(2)}) %collective-permute-start.2) | collective-permute-done | bytes 40992 | tf_op jit(solution)/shard_map/ppermute | solution.py:42
  7.1 2.0 %collective-permute-done.1.refs_2_ = bf16[40,512]{1,0:T(8,128)(2,1)S(1)} collective-permute-done((bf16[40,512]{1,0:T(8,128)(2,1)S(1)}, bf16[40,512]{1,0:T(8,128)(2,1)S(1)}, u32[]{:S(2)}, u32[]{:S(2)}) %collective-permute-start.1) | collective-permute-done | bytes 40992 | tf_op jit(solution)/shard_map/ppermute | solution.py:42
  9.1 0.5 %collective-permute-done.refs_1_ = bf16[40,512]{1,0:T(8,128)(2,1)S(1)} collective-permute-done((bf16[40,512]{1,0:T(8,128)(2,1)S(1)}, bf16[40,512]{1,0:T(8,128)(2,1)S(1)}, u32[]{:S(2)}, u32[]{:S(2)}) %collective-permute-start) | collective-permute-done | bytes 40992 | tf_op jit(solution)/shard_map/ppermute | solution.py:42
  9.6 0.5 %shard_map.74 = (bf16[48,512]{1,0:T(8,128)(2,1)S(1)}, bf16[48,512]{1,0:T(8,128)(2,1)S(1)}, bf16[48,512]{1,0:T(8,128)(2,1)S(1)}, bf16[48,512]{1,0:T(8,128)(2,1)S(...) custom-call(bf16[40,512]{1,0:T(8,128)(2,1)S(1)} %get-tuple-element.3, ...), custom_call_target="tpu_custom_call" | custom-call | tf_op jit(solution)/shard_map/pallas_call | solution.py:241
  10.1 0.1 collective-permute-start.3
  10.2 1.6 %collective-permute-start.4 = (bf16[48,512]{1,0:T(8,128)(2,1)S(1)}, bf16[48,512]{1,0:T(8,128)(2,1)S(1)}, u32[]{:S(2)}, u32[]{:S(2)}) collective-permute-start(bf16[48,512]{1,0:T(8,128)(2,1)S(1)} %get-tuple-element.40), channel_id=1, source_target_pairs={{0,8},{4,12},{8,0},{12,4},{16,24},{20,28},{24,16},{28,20},{1,9},{5... | collective-permute-start | bytes 147464 | tf_op jit(solution)/shard_map/ppermute | solution.py:42
  11.9 0.2 collective-permute-start.5
  12.1 2.6 %collective-permute-start.6 = (bf16[48,512]{1,0:T(8,128)(2,1)S(1)}, bf16[48,512]{1,0:T(8,128)(2,1)S(1)}, u32[]{:S(2)}, u32[]{:S(2)}) collective-permute-start(bf16[48,512]{1,0:T(8,128)(2,1)S(1)} %get-tuple-element.42), channel_id=1, source_target_pairs={{0,16},{4,20},{8,24},{12,28},{16,0},{20,4},{24,8},{28,12},{1,17},{... | collective-permute-start | bytes 147464 | tf_op jit(solution)/shard_map/ppermute | solution.py:42
  14.7 3.6 %collective-permute-start.8 = (bf16[48,512]{1,0:T(8,128)(2,1)S(1)}, bf16[48,512]{1,0:T(8,128)(2,1)S(1)}, u32[]{:S(2)}, u32[]{:S(2)}) collective-permute-start(bf16[48,512]{1,0:T(8,128)(2,1)S(1)} %get-tuple-element.44), channel_id=1, source_target_pairs={{0,24},{4,28},{8,16},{12,20},{16,8},{20,12},{24,0},{28,4},{1,25},{... | collective-permute-start | bytes 147464 | tf_op jit(solution)/shard_map/ppermute | solution.py:42
  18.3 0.1 collective-permute-start.9
  18.4 3.8 %shard_map.75 = (bf16[384,4096]{1,0:T(8,128)(2,1)S(1)}, bf16[384,4096]{1,0:T(8,128)(2,1)S(1)}, bf16[384,4096]{1,0:T(8,128)(2,1)S(1)}, bf16[384,384]{1,0:T(8,128)(2,1)S(1)}, bf16[384,128]{1,0:T(8,128)(2,1)S(1)}) custom-call(bf16[384,4096]{1,0:T(8,128)(2,1)} %bitcast.5, bf16[384,4096]{1,0:T(8,128)(2,1)} %bitcast.6, bf16[384,4096]{1,0:T(8,128)(2,1)} %bitcast.7, ...), custom_call_target="tpu_custom_call" | custom-call | bytes 18874368 | tf_op jit(solution)/shard_map/pallas_call | solution.py:250
  22.2 1.7 %collective-permute-done.9.refs_7_ = bf16[48,512]{1,0:T(8,128)(2,1)S(1)} collective-permute-done((bf16[48,512]{1,0:T(8,128)(2,1)S(1)}, bf16[48,512]{1,0:T(8,128)(2,1)S(1)}, u32[]{:S(2)}, u32[]{:S(2)}) %collective-permute-start.9) | collective-permute-done | bytes 49184 | tf_op jit(solution)/shard_map/ppermute | solution.py:42
  23.9 2.9 %shard_map.76 = (bf16[48,512]{1,0:T(8,128)(2,1)S(1)}, bf16[48,512]{1,0:T(8,128)(2,1)S(1)}, bf16[48,512]{1,0:T(8,128)(2,1)S(1)}, bf16[48,512]{1,0:T(8,128)(2,1)S(...) custom-call(bf16[48,512]{1,0:T(8,128)(2,1)S(1)} %get-tuple-element.3, ...), custom_call_target="tpu_custom_call" | custom-call | tf_op jit(solution)/shard_map/pallas_call | solution.py:261
  26.8 0.2 collective-permute-start.10
  27.0 1.9 %collective-permute-start.11 = (bf16[48,512]{1,0:T(8,128)(2,1)S(1)}, bf16[48,512]{1,0:T(8,128)(2,1)S(1)}, u32[]{:S(2)}, u32[]{:S(2)}) collective-permute-start(bf16[48,512]{1,0:T(8,128)(2,1)S(1)} %get-tuple-element.54), channel_id=1, source_target_pairs={{0,8},{4,12},{8,0},{12,4},{16,24},{20,28},{24,16},{28,20},{1,9},{5... | collective-permute-start | bytes 147464 | tf_op jit(solution)/shard_map/ppermute | solution.py:42
  28.9 2.8 %collective-permute-start.13 = (bf16[48,512]{1,0:T(8,128)(2,1)S(1)}, bf16[48,512]{1,0:T(8,128)(2,1)S(1)}, u32[]{:S(2)}, u32[]{:S(2)}) collective-permute-start(bf16[48,512]{1,0:T(8,128)(2,1)S(1)} %get-tuple-element.56), channel_id=1, source_target_pairs={{0,16},{4,20},{8,24},{12,28},{16,0},{20,4},{24,8},{28,12},{1,17},{... | collective-permute-start | bytes 147464 | tf_op jit(solution)/shard_map/ppermute | solution.py:42
  31.7 2.1 %collective-permute-start.15 = (bf16[48,512]{1,0:T(8,128)(2,1)S(1)}, bf16[48,512]{1,0:T(8,128)(2,1)S(1)}, u32[]{:S(2)}, u32[]{:S(2)}) collective-permute-start(bf16[48,512]{1,0:T(8,128)(2,1)S(1)} %get-tuple-element.58), channel_id=1, source_target_pairs={{0,24},{4,28},{8,16},{12,20},{16,8},{20,12},{24,0},{28,4},{1,25},{... | collective-permute-start | bytes 147464 | tf_op jit(solution)/shard_map/ppermute | solution.py:42
  33.8 1.3 %collective-permute-start.16 = (bf16[48,512]{1,0:T(8,128)(2,1)S(1)}, bf16[48,512]{1,0:T(8,128)(2,1)S(1)}, u32[]{:S(2)}, u32[]{:S(2)}) collective-permute-start(bf16[48,512]{1,0:T(8,128)(2,1)S(1)} %get-tuple-element.59), channel_id=1, source_target_pairs={{0,28},{4,24},{8,20},{12,16},{16,12},{20,8},{24,4},{28,0},{1,29},{... | collective-permute-start | bytes 147464 | tf_op jit(solution)/shard_map/ppermute | solution.py:42
  35.1 3.6 %collective-permute-done.14.refs_5_ = bf16[48,512]{1,0:T(8,128)(2,1)S(1)} collective-permute-done((bf16[48,512]{1,0:T(8,128)(2,1)S(1)}, bf16[48,512]{1,0:T(8,128)(2,1)S(1)}, u32[]{:S(2)}, u32[]{:S(2)}) %collective-permute-start.14) | collective-permute-done | bytes 49184 | tf_op jit(solution)/shard_map/ppermute | solution.py:42
  38.6 0.6 %collective-permute-done.16.refs_7_ = bf16[48,512]{1,0:T(8,128)(2,1)S(1)} collective-permute-done((bf16[48,512]{1,0:T(8,128)(2,1)S(1)}, bf16[48,512]{1,0:T(8,128)(2,1)S(1)}, u32[]{:S(2)}, u32[]{:S(2)}) %collective-permute-start.16) | collective-permute-done | bytes 49184 | tf_op jit(solution)/shard_map/ppermute | solution.py:42
  39.2 0.2 shard_map.77
  39.5 0.6 %collective-permute-start.17 = (bf16[32,512]{1,0:T(8,128)(2,1)S(1)}, bf16[32,512]{1,0:T(8,128)(2,1)S(1)}, u32[]{:S(2)}, u32[]{:S(2)}) collective-permute-start(bf16[32,512]{1,0:T(8,128)(2,1)S(1)} %get-tuple-element.62), channel_id=1, source_target_pairs={{0,1},{1,0},{2,3},{3,2},{4,5},{5,4},{6,7},{7,6},{8,9},{9,8},{10,11... | collective-permute-start | bytes 98312 | tf_op jit(solution)/shard_map/ppermute | solution.py:42
  40.1 1.5 %collective-permute-start.18 = (bf16[32,512]{1,0:T(8,128)(2,1)S(1)}, bf16[32,512]{1,0:T(8,128)(2,1)S(1)}, u32[]{:S(2)}, u32[]{:S(2)}) collective-permute-start(bf16[32,512]{1,0:T(8,128)(2,1)S(1)} %get-tuple-element.63), channel_id=1, source_target_pairs={{0,2},{1,3},{2,0},{3,1},{4,6},{5,7},{6,4},{7,5},{8,10},{9,11},{10,... | collective-permute-start | bytes 98312 | tf_op jit(solution)/shard_map/ppermute | solution.py:42
  41.6 1.4 %collective-permute-start.19 = (bf16[32,512]{1,0:T(8,128)(2,1)S(1)}, bf16[32,512]{1,0:T(8,128)(2,1)S(1)}, u32[]{:S(2)}, u32[]{:S(2)}) collective-permute-start(bf16[32,512]{1,0:T(8,128)(2,1)S(1)} %get-tuple-element.64), channel_id=1, source_target_pairs={{0,3},{1,2},{2,1},{3,0},{4,7},{5,6},{6,5},{7,4},{8,11},{9,10},{10,... | collective-permute-start | bytes 98312 | tf_op jit(solution)/shard_map/ppermute | solution.py:42
  43.0 0.4 collective-permute-done.17.refs_1_
  43.4 0.5 %collective-permute-done.18.refs_2_ = bf16[32,512]{1,0:T(8,128)(2,1)S(1)} collective-permute-done((bf16[32,512]{1,0:T(8,128)(2,1)S(1)}, bf16[32,512]{1,0:T(8,128)(2,1)S(1)}, u32[]{:S(2)}, u32[]{:S(2)}) %collective-permute-start.18) | collective-permute-done | bytes 32800 | tf_op jit(solution)/shard_map/ppermute | solution.py:42
  44.0 2.4 %collective-permute-done.19.refs_3_ = bf16[32,512]{1,0:T(8,128)(2,1)S(1)} collective-permute-done((bf16[32,512]{1,0:T(8,128)(2,1)S(1)}, bf16[32,512]{1,0:T(8,128)(2,1)S(1)}, u32[]{:S(2)}, u32[]{:S(2)}) %collective-permute-start.19) | collective-permute-done | bytes 32800 | tf_op jit(solution)/shard_map/ppermute | solution.py:42
  46.4 0.6 %shard_map.78 = bf16[4,4096]{1,0:T(4,128)(2,1)} custom-call(bf16[32,512]{1,0:T(8,128)(2,1)S(1)} %get-tuple-element.61.refs_0_, bf16[32,512]{1,0:T(8,128)(2,1)S(1)} %collective-permute-done.17.refs_1_, bf16[32,512]{1,0:T(8,128)(2,1)S(1)} %collective-permute-done.18.refs_2_, bf16[32,512]{1,0:T(8,128)(2,1)S(1)} %collective-permute-done.19.refs_3_), custom_call_target="tpu_custom_call" | custom-call | tf_op jit(solution)/shard_map/pallas_call | solution.py:278
  (14 shorter events, 0.1 us)
Async XLA Ops:
  1.1 6.0 %collective-permute-start.2 = (bf16[40,512]{1,0:T(8,128)(2,1)S(1)}, bf16[40,512]{1,0:T(8,128)(2,1)S(1)}, u32[]{:S(2)}, u32[]{:S(2)}) collective-permute-start(bf16[40,512]{1,0:T(8,128)(2,1)S(1)} %get-tuple-element.35.refs_0_), channel_id=1, source_target_pairs={{0,3},{1,2},{2,1},{3,0},{4,7},{5,6},{6,5},{7,4},{8,11},{9,10},{10,... | collective-permute-start | bytes 122888 | tf_op jit(solution)/shard_map/ppermute | solution.py:42
  5.1 4.0 %collective-permute-start.1 = (bf16[40,512]{1,0:T(8,128)(2,1)S(1)}, bf16[40,512]{1,0:T(8,128)(2,1)S(1)}, u32[]{:S(2)}, u32[]{:S(2)}) collective-permute-start(bf16[40,512]{1,0:T(8,128)(2,1)S(1)} %get-tuple-element.35.refs_0_), channel_id=1, source_target_pairs={{0,2},{1,3},{2,0},{3,1},{4,6},{5,7},{6,4},{7,5},{8,10},{9,11},{10,... | collective-permute-start | bytes 122888 | tf_op jit(solution)/shard_map/ppermute | solution.py:42
  5.6 4.0 %collective-permute-start = (bf16[40,512]{1,0:T(8,128)(2,1)S(1)}, bf16[40,512]{1,0:T(8,128)(2,1)S(1)}, u32[]{:S(2)}, u32[]{:S(2)}) collective-permute-start(bf16[40,512]{1,0:T(8,128)(2,1)S(1)} %get-tuple-element.35.refs_0_), channel_id=1, source_target_pairs={{0,1},{1,0},{2,3},{3,2},{4,5},{5,4},{6,7},{7,6},{8,9},{9,8},{10,11... | collective-permute-start | bytes 122888 | tf_op jit(solution)/shard_map/ppermute | solution.py:42
  10.1 4.5 %collective-permute-start.3 = (bf16[48,512]{1,0:T(8,128)(2,1)S(1)}, bf16[48,512]{1,0:T(8,128)(2,1)S(1)}, u32[]{:S(2)}, u32[]{:S(2)}) collective-permute-start(bf16[48,512]{1,0:T(8,128)(2,1)S(1)} %get-tuple-element.39), channel_id=1, source_target_pairs={{0,4},{4,0},{8,12},{12,8},{16,20},{20,16},{24,28},{28,24},{1,5},{5... | collective-permute-start | bytes 147464 | tf_op jit(solution)/shard_map/ppermute | solution.py:42
  10.2 8.1 %collective-permute-start.4 = (bf16[48,512]{1,0:T(8,128)(2,1)S(1)}, bf16[48,512]{1,0:T(8,128)(2,1)S(1)}, u32[]{:S(2)}, u32[]{:S(2)}) collective-permute-start(bf16[48,512]{1,0:T(8,128)(2,1)S(1)} %get-tuple-element.40), channel_id=1, source_target_pairs={{0,8},{4,12},{8,0},{12,4},{16,24},{20,28},{24,16},{28,20},{1,9},{5... | collective-permute-start | bytes 147464 | tf_op jit(solution)/shard_map/ppermute | solution.py:42
  11.9 10.3 %collective-permute-start.5 = (bf16[48,512]{1,0:T(8,128)(2,1)S(1)}, bf16[48,512]{1,0:T(8,128)(2,1)S(1)}, u32[]{:S(2)}, u32[]{:S(2)}) collective-permute-start(bf16[48,512]{1,0:T(8,128)(2,1)S(1)} %get-tuple-element.41), channel_id=1, source_target_pairs={{0,12},{4,8},{8,4},{12,0},{16,28},{20,24},{24,20},{28,16},{1,13},{... | collective-permute-start | bytes 147464 | tf_op jit(solution)/shard_map/ppermute | solution.py:42
  12.1 10.1 %collective-permute-start.6 = (bf16[48,512]{1,0:T(8,128)(2,1)S(1)}, bf16[48,512]{1,0:T(8,128)(2,1)S(1)}, u32[]{:S(2)}, u32[]{:S(2)}) collective-permute-start(bf16[48,512]{1,0:T(8,128)(2,1)S(1)} %get-tuple-element.42), channel_id=1, source_target_pairs={{0,16},{4,20},{8,24},{12,28},{16,0},{20,4},{24,8},{28,12},{1,17},{... | collective-permute-start | bytes 147464 | tf_op jit(solution)/shard_map/ppermute | solution.py:42
  14.6 7.5 %collective-permute-start.7 = (bf16[48,512]{1,0:T(8,128)(2,1)S(1)}, bf16[48,512]{1,0:T(8,128)(2,1)S(1)}, u32[]{:S(2)}, u32[]{:S(2)}) collective-permute-start(bf16[48,512]{1,0:T(8,128)(2,1)S(1)} %get-tuple-element.43), channel_id=1, source_target_pairs={{0,20},{4,16},{8,28},{12,24},{16,4},{20,0},{24,12},{28,8},{1,21},{... | collective-permute-start | bytes 147464 | tf_op jit(solution)/shard_map/ppermute | solution.py:42
  14.7 7.5 %collective-permute-start.8 = (bf16[48,512]{1,0:T(8,128)(2,1)S(1)}, bf16[48,512]{1,0:T(8,128)(2,1)S(1)}, u32[]{:S(2)}, u32[]{:S(2)}) collective-permute-start(bf16[48,512]{1,0:T(8,128)(2,1)S(1)} %get-tuple-element.44), channel_id=1, source_target_pairs={{0,24},{4,28},{8,16},{12,20},{16,8},{20,12},{24,0},{28,4},{1,25},{... | collective-permute-start | bytes 147464 | tf_op jit(solution)/shard_map/ppermute | solution.py:42
  18.3 5.6 %collective-permute-start.9 = (bf16[48,512]{1,0:T(8,128)(2,1)S(1)}, bf16[48,512]{1,0:T(8,128)(2,1)S(1)}, u32[]{:S(2)}, u32[]{:S(2)}) collective-permute-start(bf16[48,512]{1,0:T(8,128)(2,1)S(1)} %get-tuple-element.45), channel_id=1, source_target_pairs={{0,28},{4,24},{8,20},{12,16},{16,12},{20,8},{24,4},{28,0},{1,29},{... | collective-permute-start | bytes 147464 | tf_op jit(solution)/shard_map/ppermute | solution.py:42
  26.8 4.9 %collective-permute-start.10 = (bf16[48,512]{1,0:T(8,128)(2,1)S(1)}, bf16[48,512]{1,0:T(8,128)(2,1)S(1)}, u32[]{:S(2)}, u32[]{:S(2)}) collective-permute-start(bf16[48,512]{1,0:T(8,128)(2,1)S(1)} %get-tuple-element.53), channel_id=1, source_target_pairs={{0,4},{4,0},{8,12},{12,8},{16,20},{20,16},{24,28},{28,24},{1,5},{5... | collective-permute-start | bytes 147464 | tf_op jit(solution)/shard_map/ppermute | solution.py:42
  27.0 6.8 %collective-permute-start.11 = (bf16[48,512]{1,0:T(8,128)(2,1)S(1)}, bf16[48,512]{1,0:T(8,128)(2,1)S(1)}, u32[]{:S(2)}, u32[]{:S(2)}) collective-permute-start(bf16[48,512]{1,0:T(8,128)(2,1)S(1)} %get-tuple-element.54), channel_id=1, source_target_pairs={{0,8},{4,12},{8,0},{12,4},{16,24},{20,28},{24,16},{28,20},{1,9},{5... | collective-permute-start | bytes 147464 | tf_op jit(solution)/shard_map/ppermute | solution.py:42
  28.9 6.2 %collective-permute-start.12 = (bf16[48,512]{1,0:T(8,128)(2,1)S(1)}, bf16[48,512]{1,0:T(8,128)(2,1)S(1)}, u32[]{:S(2)}, u32[]{:S(2)}) collective-permute-start(bf16[48,512]{1,0:T(8,128)(2,1)S(1)} %get-tuple-element.55), channel_id=1, source_target_pairs={{0,12},{4,8},{8,4},{12,0},{16,28},{20,24},{24,20},{28,16},{1,13},{... | collective-permute-start | bytes 147464 | tf_op jit(solution)/shard_map/ppermute | solution.py:42
  28.9 6.2 %collective-permute-start.13 = (bf16[48,512]{1,0:T(8,128)(2,1)S(1)}, bf16[48,512]{1,0:T(8,128)(2,1)S(1)}, u32[]{:S(2)}, u32[]{:S(2)}) collective-permute-start(bf16[48,512]{1,0:T(8,128)(2,1)S(1)} %get-tuple-element.56), channel_id=1, source_target_pairs={{0,16},{4,20},{8,24},{12,28},{16,0},{20,4},{24,8},{28,12},{1,17},{... | collective-permute-start | bytes 147464 | tf_op jit(solution)/shard_map/ppermute | solution.py:42
  31.7 7.0 %collective-permute-start.14 = (bf16[48,512]{1,0:T(8,128)(2,1)S(1)}, bf16[48,512]{1,0:T(8,128)(2,1)S(1)}, u32[]{:S(2)}, u32[]{:S(2)}) collective-permute-start(bf16[48,512]{1,0:T(8,128)(2,1)S(1)} %get-tuple-element.57), channel_id=1, source_target_pairs={{0,20},{4,16},{8,28},{12,24},{16,4},{20,0},{24,12},{28,8},{1,21},{... | collective-permute-start | bytes 147464 | tf_op jit(solution)/shard_map/ppermute | solution.py:42
  31.7 7.0 %collective-permute-start.15 = (bf16[48,512]{1,0:T(8,128)(2,1)S(1)}, bf16[48,512]{1,0:T(8,128)(2,1)S(1)}, u32[]{:S(2)}, u32[]{:S(2)}) collective-permute-start(bf16[48,512]{1,0:T(8,128)(2,1)S(1)} %get-tuple-element.58), channel_id=1, source_target_pairs={{0,24},{4,28},{8,16},{12,20},{16,8},{20,12},{24,0},{28,4},{1,25},{... | collective-permute-start | bytes 147464 | tf_op jit(solution)/shard_map/ppermute | solution.py:42
  33.8 5.4 %collective-permute-start.16 = (bf16[48,512]{1,0:T(8,128)(2,1)S(1)}, bf16[48,512]{1,0:T(8,128)(2,1)S(1)}, u32[]{:S(2)}, u32[]{:S(2)}) collective-permute-start(bf16[48,512]{1,0:T(8,128)(2,1)S(1)} %get-tuple-element.59), channel_id=1, source_target_pairs={{0,28},{4,24},{8,20},{12,16},{16,12},{20,8},{24,4},{28,0},{1,29},{... | collective-permute-start | bytes 147464 | tf_op jit(solution)/shard_map/ppermute | solution.py:42
  39.5 4.0 %collective-permute-start.17 = (bf16[32,512]{1,0:T(8,128)(2,1)S(1)}, bf16[32,512]{1,0:T(8,128)(2,1)S(1)}, u32[]{:S(2)}, u32[]{:S(2)}) collective-permute-start(bf16[32,512]{1,0:T(8,128)(2,1)S(1)} %get-tuple-element.62), channel_id=1, source_target_pairs={{0,1},{1,0},{2,3},{3,2},{4,5},{5,4},{6,7},{7,6},{8,9},{9,8},{10,11... | collective-permute-start | bytes 98312 | tf_op jit(solution)/shard_map/ppermute | solution.py:42
  40.1 3.9 %collective-permute-start.18 = (bf16[32,512]{1,0:T(8,128)(2,1)S(1)}, bf16[32,512]{1,0:T(8,128)(2,1)S(1)}, u32[]{:S(2)}, u32[]{:S(2)}) collective-permute-start(bf16[32,512]{1,0:T(8,128)(2,1)S(1)} %get-tuple-element.63), channel_id=1, source_target_pairs={{0,2},{1,3},{2,0},{3,1},{4,6},{5,7},{6,4},{7,5},{8,10},{9,11},{10,... | collective-permute-start | bytes 98312 | tf_op jit(solution)/shard_map/ppermute | solution.py:42
  41.6 4.8 %collective-permute-start.19 = (bf16[32,512]{1,0:T(8,128)(2,1)S(1)}, bf16[32,512]{1,0:T(8,128)(2,1)S(1)}, u32[]{:S(2)}, u32[]{:S(2)}) collective-permute-start(bf16[32,512]{1,0:T(8,128)(2,1)S(1)} %get-tuple-element.64), channel_id=1, source_target_pairs={{0,3},{1,2},{2,1},{3,0},{4,7},{5,6},{6,5},{7,4},{8,11},{9,10},{10,... | collective-permute-start | bytes 98312 | tf_op jit(solution)/shard_map/ppermute | solution.py:42
where the time goes:
time: 47.3 us; the launch traced here: 47 us
  starting transfers between devices  24.7 us (52%)
  waiting for transfers between devices  13.1 us (28%)
  Pallas kernels  9.14 us (19%)
    ppermute x20, starting transfers between devices, swap(): lax.ppermute(xs[j], axis, [(i, partner(i, j, n)) for i in range(n)])  24.7 us
    ppermute x20, waiting for transfers between devices, swap(): lax.ppermute(xs[j], axis, [(i, partner(i, j, n)) for i in range(n)])  13.1 us
    pallas_call x1, Pallas kernels, body(): call(functools.partial(fetch_kernel, n_expert, topk), [shape(*w.shape) fo...  3.78 us
    pallas_call x1, Pallas kernels, body(): call(functools.partial(expert_kernel, n_expert), [shape(slots * CHUNKS, l...  2.86 us
    pallas_call x1, Pallas kernels, body(): call(pack_kernel, [shape(per + extra, lanes), table, table], [hbm] * 4, (...  1.08 us
  transfers between devices with their start and end apart: 20, of which 9 were waited for; matrix products, arithmetic and copies ran while one was open for 0% of the time, Pallas kernels for 8%

commit v1 on v0

--- a/solution.py
+++ b/solution.py
@@ -11,6 +11,7 @@
 BF16, F32, I32 = jnp.bfloat16, jnp.float32, jnp.int32
 CHUNKS = 8
 LANES = 128
+PARTS = 4
 
 
 def iota(shape, dim):
@@ -135,9 +136,9 @@
     x = mm(order_ref[...], y_ref[...]).astype(BF16)
     for c in range(CHUNKS):
         x_ref[:, c * lanes:(c + 1) * lanes] = x[c * count:(c + 1) * count, :]
-    gate = mm(x_ref[...], gate_ref[...], nt)
-    up = mm(x_ref[...], up_ref[...], nt)
-    hidden = (gate / (1.0 + jnp.exp(-gate)) * up).astype(BF16)
+    gate = mm(gate_ref[...], x_ref[...], nt)
+    up = mm(up_ref[...], x_ref[...], nt)
+    hidden = (gate / (1.0 + jnp.exp(-gate)) * up).T.astype(BF16)
     for c in range(CHUNKS):
         value = mm(hidden, down_ref[:, c * lanes:(c + 1) * lanes]).astype(BF16)
         y_ref[c * count:(c + 1) * count, :] = value
@@ -188,7 +189,12 @@
     ins, pick_ref, small_ref, outs, order_ref, mix_ref, sems = (
         refs[:3], refs[3], refs[4], refs[5:8], refs[8], refs[9], refs[10]
     )
-    copies = [pltpu.make_async_copy(a, b, sems.at[i]) for i, (a, b) in enumerate(zip(ins, outs))]
+    copies = []
+    for i, (a, b) in enumerate(zip(ins, outs)):
+        part = a.shape[0] // PARTS
+        for p in range(PARTS):
+            rows = pl.ds(p * part, part)
+            copies.append(pltpu.make_async_copy(a.at[rows], b.at[rows], sems.at[i * PARTS + p]))
     for copy in copies:
         copy.start()
     total, columns = pick_ref.shape
@@ -210,7 +216,7 @@
     count, width = tokens.shape
     topk = expert_ids.shape[1]
     group = count * n_dp
-    assert group <= LANES and n_expert < 256 and width % (CHUNKS * LANES) == 0
+    assert group <= LANES and w_gate.shape[1] % (16 * PARTS) == 0 and n_expert < 256 and width % (CHUNKS * LANES) == 0
     assert width >= 2 * CHUNKS * LANES and placement.shape[1] <= 8
     first = max(2, group * topk // n_expert)
     slots = first + max(1, first // 2)
@@ -251,7 +257,7 @@
         functools.partial(fetch_kernel, n_expert, topk),
         [shape(*w.shape) for w in weights] + [shape(total, total), shape(total, columns)],
         [hbm] * 3 + [vmem] * 2,
-        (pltpu.SemaphoreType.DMA((3,)),),
+        (pltpu.SemaphoreType.DMA((3 * PARTS,)),),
         limit=48 << 20 if big else 16 << 20,
         cost_estimate=pl.CostEstimate(
             flops=0, bytes_accessed=sum(4 * w.size for w in weights), transcendentals=0

time: 47.3 us -> 47.4 us (level)
  no operation moved by 1% of the time
where the time goes in v1:
time: 47.4 us; the launch traced here: 47.1 us
  starting transfers between devices  24.7 us (52%)
  waiting for transfers between devices  13 us (27%)
  Pallas kernels  9.27 us (20%)
    ppermute x20, starting transfers between devices, swap(): lax.ppermute(xs[j], axis, [(i, partner(i, j, n)) for i in range(n)])  24.7 us
    ppermute x20, waiting for transfers between devices, swap(): lax.ppermute(xs[j], axis, [(i, partner(i, j, n)) for i in range(n)])  13 us
    pallas_call x1, Pallas kernels, body(): call(functools.partial(fetch_kernel, n_expert, topk), [shape(*w.shape) fo...  3.79 us
    pallas_call x1, Pallas kernels, body(): call(functools.partial(expert_kernel, n_expert), [shape(slots * CHUNKS, l...  2.98 us
    pallas_call x1, Pallas kernels, body(): call(pack_kernel, [shape(per + extra, lanes), table, table], [hbm] * 4, (...  1.08 us
  transfers between devices with their start and end apart: 20, of which 9 were waited for; matrix products, arithmetic and copies ran while one was open for 0% of the time, Pallas kernels for 8%

profile of v1, /device:TPU:0, one launch (start us, length us, event | category | flops | bytes accessed | tf_op | source)
XLA Modules:
  0.0 47.1 jit_solution(17893724011745919566)
XLA Ops:
  0.0 1.1 %shard_map.73 = (bf16[40,512]{1,0:T(8,128)(2,1)S(1)}, bf16[128,128]{1,0:T(8,128)(2,1)S(1)}, bf16[128,128]{1,0:T(8,128)(2,1)S(1)}) custom-call(bf16[4,4096]{1,0:T(4,128)(2,1)} %tok_hbm.1, s32[2,4]{1,0:T(2,128)} %bitcast.8, bf16[2,4]{1,0:T(2,128)(2,1)} %bitcast.9, s32[2,2]{1,0:T(2,128)} %place_hbm.1), custom_call_target="tpu_custom_call" | custom-call | tf_op jit(solution)/shard_map/pallas_call | solution.py:233
  1.1 4.0 %collective-permute-start.2 = (bf16[40,512]{1,0:T(8,128)(2,1)S(1)}, bf16[40,512]{1,0:T(8,128)(2,1)S(1)}, u32[]{:S(2)}, u32[]{:S(2)}) collective-permute-start(bf16[40,512]{1,0:T(8,128)(2,1)S(1)} %get-tuple-element.35.refs_0_), channel_id=1, source_target_pairs={{0,3},{1,2},{2,1},{3,0},{4,7},{5,6},{6,5},{7,4},{8,11},{9,10},{10,... | collective-permute-start | bytes 122888 | tf_op jit(solution)/shard_map/ppermute | solution.py:43
  5.1 0.5 %collective-permute-start.1 = (bf16[40,512]{1,0:T(8,128)(2,1)S(1)}, bf16[40,512]{1,0:T(8,128)(2,1)S(1)}, u32[]{:S(2)}, u32[]{:S(2)}) collective-permute-start(bf16[40,512]{1,0:T(8,128)(2,1)S(1)} %get-tuple-element.35.refs_0_), channel_id=1, source_target_pairs={{0,2},{1,3},{2,0},{3,1},{4,6},{5,7},{6,4},{7,5},{8,10},{9,11},{10,... | collective-permute-start | bytes 122888 | tf_op jit(solution)/shard_map/ppermute | solution.py:43
  5.6 0.1 collective-permute-start
  5.7 1.3 %collective-permute-done.2.refs_3_ = bf16[40,512]{1,0:T(8,128)(2,1)S(1)} collective-permute-done((bf16[40,512]{1,0:T(8,128)(2,1)S(1)}, bf16[40,512]{1,0:T(8,128)(2,1)S(1)}, u32[]{:S(2)}, u32[]{:S(2)}) %collective-permute-start.2) | collective-permute-done | bytes 40992 | tf_op jit(solution)/shard_map/ppermute | solution.py:43
  7.1 2.0 %collective-permute-done.1.refs_2_ = bf16[40,512]{1,0:T(8,128)(2,1)S(1)} collective-permute-done((bf16[40,512]{1,0:T(8,128)(2,1)S(1)}, bf16[40,512]{1,0:T(8,128)(2,1)S(1)}, u32[]{:S(2)}, u32[]{:S(2)}) %collective-permute-start.1) | collective-permute-done | bytes 40992 | tf_op jit(solution)/shard_map/ppermute | solution.py:43
  9.1 0.5 %collective-permute-done.refs_1_ = bf16[40,512]{1,0:T(8,128)(2,1)S(1)} collective-permute-done((bf16[40,512]{1,0:T(8,128)(2,1)S(1)}, bf16[40,512]{1,0:T(8,128)(2,1)S(1)}, u32[]{:S(2)}, u32[]{:S(2)}) %collective-permute-start) | collective-permute-done | bytes 40992 | tf_op jit(solution)/shard_map/ppermute | solution.py:43
  9.6 0.5 %shard_map.74 = (bf16[48,512]{1,0:T(8,128)(2,1)S(1)}, bf16[48,512]{1,0:T(8,128)(2,1)S(1)}, bf16[48,512]{1,0:T(8,128)(2,1)S(1)}, bf16[48,512]{1,0:T(8,128)(2,1)S(...) custom-call(bf16[40,512]{1,0:T(8,128)(2,1)S(1)} %get-tuple-element.3, ...), custom_call_target="tpu_custom_call" | custom-call | tf_op jit(solution)/shard_map/pallas_call | solution.py:247
  10.1 0.1 collective-permute-start.3
  10.2 1.6 %collective-permute-start.4 = (bf16[48,512]{1,0:T(8,128)(2,1)S(1)}, bf16[48,512]{1,0:T(8,128)(2,1)S(1)}, u32[]{:S(2)}, u32[]{:S(2)}) collective-permute-start(bf16[48,512]{1,0:T(8,128)(2,1)S(1)} %get-tuple-element.40), channel_id=1, source_target_pairs={{0,8},{4,12},{8,0},{12,4},{16,24},{20,28},{24,16},{28,20},{1,9},{5... | collective-permute-start | bytes 147464 | tf_op jit(solution)/shard_map/ppermute | solution.py:43
  11.9 0.2 collective-permute-start.5
  12.1 2.6 %collective-permute-start.6 = (bf16[48,512]{1,0:T(8,128)(2,1)S(1)}, bf16[48,512]{1,0:T(8,128)(2,1)S(1)}, u32[]{:S(2)}, u32[]{:S(2)}) collective-permute-start(bf16[48,512]{1,0:T(8,128)(2,1)S(1)} %get-tuple-element.42), channel_id=1, source_target_pairs={{0,16},{4,20},{8,24},{12,28},{16,0},{20,4},{24,8},{28,12},{1,17},{... | collective-permute-start | bytes 147464 | tf_op jit(solution)/shard_map/ppermute | solution.py:43
  14.7 3.6 %collective-permute-start.8 = (bf16[48,512]{1,0:T(8,128)(2,1)S(1)}, bf16[48,512]{1,0:T(8,128)(2,1)S(1)}, u32[]{:S(2)}, u32[]{:S(2)}) collective-permute-start(bf16[48,512]{1,0:T(8,128)(2,1)S(1)} %get-tuple-element.44), channel_id=1, source_target_pairs={{0,24},{4,28},{8,16},{12,20},{16,8},{20,12},{24,0},{28,4},{1,25},{... | collective-permute-start | bytes 147464 | tf_op jit(solution)/shard_map/ppermute | solution.py:43
  18.3 0.1 collective-permute-start.9
  18.4 3.8 %shard_map.75 = (bf16[384,4096]{1,0:T(8,128)(2,1)S(1)}, bf16[384,4096]{1,0:T(8,128)(2,1)S(1)}, bf16[384,4096]{1,0:T(8,128)(2,1)S(1)}, bf16[384,384]{1,0:T(8,128)(2,1)S(1)}, bf16[384,128]{1,0:T(8,128)(2,1)S(1)}) custom-call(bf16[384,4096]{1,0:T(8,128)(2,1)} %bitcast.5, bf16[384,4096]{1,0:T(8,128)(2,1)} %bitcast.6, bf16[384,4096]{1,0:T(8,128)(2,1)} %bitcast.7, ...), custom_call_target="tpu_custom_call" | custom-call | bytes 18874368 | tf_op jit(solution)/shard_map/pallas_call | solution.py:256
  22.2 1.7 %collective-permute-done.9.refs_7_ = bf16[48,512]{1,0:T(8,128)(2,1)S(1)} collective-permute-done((bf16[48,512]{1,0:T(8,128)(2,1)S(1)}, bf16[48,512]{1,0:T(8,128)(2,1)S(1)}, u32[]{:S(2)}, u32[]{:S(2)}) %collective-permute-start.9) | collective-permute-done | bytes 49184 | tf_op jit(solution)/shard_map/ppermute | solution.py:43
  23.9 3.0 %shard_map.76 = (bf16[48,512]{1,0:T(8,128)(2,1)S(1)}, bf16[48,512]{1,0:T(8,128)(2,1)S(1)}, bf16[48,512]{1,0:T(8,128)(2,1)S(1)}, bf16[48,512]{1,0:T(8,128)(2,1)S(...) custom-call(bf16[48,512]{1,0:T(8,128)(2,1)S(1)} %get-tuple-element.3, ...), custom_call_target="tpu_custom_call" | custom-call | tf_op jit(solution)/shard_map/pallas_call | solution.py:267
  26.9 0.2 collective-permute-start.10
  27.1 1.9 %collective-permute-start.11 = (bf16[48,512]{1,0:T(8,128)(2,1)S(1)}, bf16[48,512]{1,0:T(8,128)(2,1)S(1)}, u32[]{:S(2)}, u32[]{:S(2)}) collective-permute-start(bf16[48,512]{1,0:T(8,128)(2,1)S(1)} %get-tuple-element.54), channel_id=1, source_target_pairs={{0,8},{4,12},{8,0},{12,4},{16,24},{20,28},{24,16},{28,20},{1,9},{5... | collective-permute-start | bytes 147464 | tf_op jit(solution)/shard_map/ppermute | solution.py:43
  29.0 2.8 %collective-permute-start.13 = (bf16[48,512]{1,0:T(8,128)(2,1)S(1)}, bf16[48,512]{1,0:T(8,128)(2,1)S(1)}, u32[]{:S(2)}, u32[]{:S(2)}) collective-permute-start(bf16[48,512]{1,0:T(8,128)(2,1)S(1)} %get-tuple-element.56), channel_id=1, source_target_pairs={{0,16},{4,20},{8,24},{12,28},{16,0},{20,4},{24,8},{28,12},{1,17},{... | collective-permute-start | bytes 147464 | tf_op jit(solution)/shard_map/ppermute | solution.py:43
  31.8 2.1 %collective-permute-start.15 = (bf16[48,512]{1,0:T(8,128)(2,1)S(1)}, bf16[48,512]{1,0:T(8,128)(2,1)S(1)}, u32[]{:S(2)}, u32[]{:S(2)}) collective-permute-start(bf16[48,512]{1,0:T(8,128)(2,1)S(1)} %get-tuple-element.58), channel_id=1, source_target_pairs={{0,24},{4,28},{8,16},{12,20},{16,8},{20,12},{24,0},{28,4},{1,25},{... | collective-permute-start | bytes 147464 | tf_op jit(solution)/shard_map/ppermute | solution.py:43
  33.9 1.3 %collective-permute-start.16 = (bf16[48,512]{1,0:T(8,128)(2,1)S(1)}, bf16[48,512]{1,0:T(8,128)(2,1)S(1)}, u32[]{:S(2)}, u32[]{:S(2)}) collective-permute-start(bf16[48,512]{1,0:T(8,128)(2,1)S(1)} %get-tuple-element.59), channel_id=1, source_target_pairs={{0,28},{4,24},{8,20},{12,16},{16,12},{20,8},{24,4},{28,0},{1,29},{... | collective-permute-start | bytes 147464 | tf_op jit(solution)/shard_map/ppermute | solution.py:43
  35.2 3.6 %collective-permute-done.14.refs_5_ = bf16[48,512]{1,0:T(8,128)(2,1)S(1)} collective-permute-done((bf16[48,512]{1,0:T(8,128)(2,1)S(1)}, bf16[48,512]{1,0:T(8,128)(2,1)S(1)}, u32[]{:S(2)}, u32[]{:S(2)}) %collective-permute-start.14) | collective-permute-done | bytes 49184 | tf_op jit(solution)/shard_map/ppermute | solution.py:43
  38.8 0.6 %collective-permute-done.16.refs_7_ = bf16[48,512]{1,0:T(8,128)(2,1)S(1)} collective-permute-done((bf16[48,512]{1,0:T(8,128)(2,1)S(1)}, bf16[48,512]{1,0:T(8,128)(2,1)S(1)}, u32[]{:S(2)}, u32[]{:S(2)}) %collective-permute-start.16) | collective-permute-done | bytes 49184 | tf_op jit(solution)/shard_map/ppermute | solution.py:43
  39.3 0.2 shard_map.77
  39.6 0.6 %collective-permute-start.17 = (bf16[32,512]{1,0:T(8,128)(2,1)S(1)}, bf16[32,512]{1,0:T(8,128)(2,1)S(1)}, u32[]{:S(2)}, u32[]{:S(2)}) collective-permute-start(bf16[32,512]{1,0:T(8,128)(2,1)S(1)} %get-tuple-element.62), channel_id=1, source_target_pairs={{0,1},{1,0},{2,3},{3,2},{4,5},{5,4},{6,7},{7,6},{8,9},{9,8},{10,11... | collective-permute-start | bytes 98312 | tf_op jit(solution)/shard_map/ppermute | solution.py:43
  40.2 1.5 %collective-permute-start.18 = (bf16[32,512]{1,0:T(8,128)(2,1)S(1)}, bf16[32,512]{1,0:T(8,128)(2,1)S(1)}, u32[]{:S(2)}, u32[]{:S(2)}) collective-permute-start(bf16[32,512]{1,0:T(8,128)(2,1)S(1)} %get-tuple-element.63), channel_id=1, source_target_pairs={{0,2},{1,3},{2,0},{3,1},{4,6},{5,7},{6,4},{7,5},{8,10},{9,11},{10,... | collective-permute-start | bytes 98312 | tf_op jit(solution)/shard_map/ppermute | solution.py:43
  41.7 1.4 %collective-permute-start.19 = (bf16[32,512]{1,0:T(8,128)(2,1)S(1)}, bf16[32,512]{1,0:T(8,128)(2,1)S(1)}, u32[]{:S(2)}, u32[]{:S(2)}) collective-permute-start(bf16[32,512]{1,0:T(8,128)(2,1)S(1)} %get-tuple-element.64), channel_id=1, source_target_pairs={{0,3},{1,2},{2,1},{3,0},{4,7},{5,6},{6,5},{7,4},{8,11},{9,10},{10,... | collective-permute-start | bytes 98312 | tf_op jit(solution)/shard_map/ppermute | solution.py:43
  43.1 0.4 collective-permute-done.17.refs_1_
  43.6 0.5 %collective-permute-done.18.refs_2_ = bf16[32,512]{1,0:T(8,128)(2,1)S(1)} collective-permute-done((bf16[32,512]{1,0:T(8,128)(2,1)S(1)}, bf16[32,512]{1,0:T(8,128)(2,1)S(1)}, u32[]{:S(2)}, u32[]{:S(2)}) %collective-permute-start.18) | collective-permute-done | bytes 32800 | tf_op jit(solution)/shard_map/ppermute | solution.py:43
  44.1 2.4 %collective-permute-done.19.refs_3_ = bf16[32,512]{1,0:T(8,128)(2,1)S(1)} collective-permute-done((bf16[32,512]{1,0:T(8,128)(2,1)S(1)}, bf16[32,512]{1,0:T(8,128)(2,1)S(1)}, u32[]{:S(2)}, u32[]{:S(2)}) %collective-permute-start.19) | collective-permute-done | bytes 32800 | tf_op jit(solution)/shard_map/ppermute | solution.py:43
  46.5 0.6 %shard_map.78 = bf16[4,4096]{1,0:T(4,128)(2,1)} custom-call(bf16[32,512]{1,0:T(8,128)(2,1)S(1)} %get-tuple-element.61.refs_0_, bf16[32,512]{1,0:T(8,128)(2,1)S(1)} %collective-permute-done.17.refs_1_, bf16[32,512]{1,0:T(8,128)(2,1)S(1)} %collective-permute-done.18.refs_2_, bf16[32,512]{1,0:T(8,128)(2,1)S(1)} %collective-permute-done.19.refs_3_), custom_call_target="tpu_custom_call" | custom-call | tf_op jit(solution)/shard_map/pallas_call | solution.py:284
  (14 shorter events, 0.1 us)
Async XLA Ops:
  1.1 6.0 %collective-permute-start.2 = (bf16[40,512]{1,0:T(8,128)(2,1)S(1)}, bf16[40,512]{1,0:T(8,128)(2,1)S(1)}, u32[]{:S(2)}, u32[]{:S(2)}) collective-permute-start(bf16[40,512]{1,0:T(8,128)(2,1)S(1)} %get-tuple-element.35.refs_0_), channel_id=1, source_target_pairs={{0,3},{1,2},{2,1},{3,0},{4,7},{5,6},{6,5},{7,4},{8,11},{9,10},{10,... | collective-permute-start | bytes 122888 | tf_op jit(solution)/shard_map/ppermute | solution.py:43
  5.1 4.0 %collective-permute-start.1 = (bf16[40,512]{1,0:T(8,128)(2,1)S(1)}, bf16[40,512]{1,0:T(8,128)(2,1)S(1)}, u32[]{:S(2)}, u32[]{:S(2)}) collective-permute-start(bf16[40,512]{1,0:T(8,128)(2,1)S(1)} %get-tuple-element.35.refs_0_), channel_id=1, source_target_pairs={{0,2},{1,3},{2,0},{3,1},{4,6},{5,7},{6,4},{7,5},{8,10},{9,11},{10,... | collective-permute-start | bytes 122888 | tf_op jit(solution)/shard_map/ppermute | solution.py:43
  5.6 4.0 %collective-permute-start = (bf16[40,512]{1,0:T(8,128)(2,1)S(1)}, bf16[40,512]{1,0:T(8,128)(2,1)S(1)}, u32[]{:S(2)}, u32[]{:S(2)}) collective-permute-start(bf16[40,512]{1,0:T(8,128)(2,1)S(1)} %get-tuple-element.35.refs_0_), channel_id=1, source_target_pairs={{0,1},{1,0},{2,3},{3,2},{4,5},{5,4},{6,7},{7,6},{8,9},{9,8},{10,11... | collective-permute-start | bytes 122888 | tf_op jit(solution)/shard_map/ppermute | solution.py:43
  10.1 4.5 %collective-permute-start.3 = (bf16[48,512]{1,0:T(8,128)(2,1)S(1)}, bf16[48,512]{1,0:T(8,128)(2,1)S(1)}, u32[]{:S(2)}, u32[]{:S(2)}) collective-permute-start(bf16[48,512]{1,0:T(8,128)(2,1)S(1)} %get-tuple-element.39), channel_id=1, source_target_pairs={{0,4},{4,0},{8,12},{12,8},{16,20},{20,16},{24,28},{28,24},{1,5},{5... | collective-permute-start | bytes 147464 | tf_op jit(solution)/shard_map/ppermute | solution.py:43
  10.2 8.1 %collective-permute-start.4 = (bf16[48,512]{1,0:T(8,128)(2,1)S(1)}, bf16[48,512]{1,0:T(8,128)(2,1)S(1)}, u32[]{:S(2)}, u32[]{:S(2)}) collective-permute-start(bf16[48,512]{1,0:T(8,128)(2,1)S(1)} %get-tuple-element.40), channel_id=1, source_target_pairs={{0,8},{4,12},{8,0},{12,4},{16,24},{20,28},{24,16},{28,20},{1,9},{5... | collective-permute-start | bytes 147464 | tf_op jit(solution)/shard_map/ppermute | solution.py:43
  11.9 10.3 %collective-permute-start.5 = (bf16[48,512]{1,0:T(8,128)(2,1)S(1)}, bf16[48,512]{1,0:T(8,128)(2,1)S(1)}, u32[]{:S(2)}, u32[]{:S(2)}) collective-permute-start(bf16[48,512]{1,0:T(8,128)(2,1)S(1)} %get-tuple-element.41), channel_id=1, source_target_pairs={{0,12},{4,8},{8,4},{12,0},{16,28},{20,24},{24,20},{28,16},{1,13},{... | collective-permute-start | bytes 147464 | tf_op jit(solution)/shard_map/ppermute | solution.py:43
  12.1 10.1 %collective-permute-start.6 = (bf16[48,512]{1,0:T(8,128)(2,1)S(1)}, bf16[48,512]{1,0:T(8,128)(2,1)S(1)}, u32[]{:S(2)}, u32[]{:S(2)}) collective-permute-start(bf16[48,512]{1,0:T(8,128)(2,1)S(1)} %get-tuple-element.42), channel_id=1, source_target_pairs={{0,16},{4,20},{8,24},{12,28},{16,0},{20,4},{24,8},{28,12},{1,17},{... | collective-permute-start | bytes 147464 | tf_op jit(solution)/shard_map/ppermute | solution.py:43
  14.6 7.6 %collective-permute-start.7 = (bf16[48,512]{1,0:T(8,128)(2,1)S(1)}, bf16[48,512]{1,0:T(8,128)(2,1)S(1)}, u32[]{:S(2)}, u32[]{:S(2)}) collective-permute-start(bf16[48,512]{1,0:T(8,128)(2,1)S(1)} %get-tuple-element.43), channel_id=1, source_target_pairs={{0,20},{4,16},{8,28},{12,24},{16,4},{20,0},{24,12},{28,8},{1,21},{... | collective-permute-start | bytes 147464 | tf_op jit(solution)/shard_map/ppermute | solution.py:43
  14.7 7.6 %collective-permute-start.8 = (bf16[48,512]{1,0:T(8,128)(2,1)S(1)}, bf16[48,512]{1,0:T(8,128)(2,1)S(1)}, u32[]{:S(2)}, u32[]{:S(2)}) collective-permute-start(bf16[48,512]{1,0:T(8,128)(2,1)S(1)} %get-tuple-element.44), channel_id=1, source_target_pairs={{0,24},{4,28},{8,16},{12,20},{16,8},{20,12},{24,0},{28,4},{1,25},{... | collective-permute-start | bytes 147464 | tf_op jit(solution)/shard_map/ppermute | solution.py:43
  18.3 5.6 %collective-permute-start.9 = (bf16[48,512]{1,0:T(8,128)(2,1)S(1)}, bf16[48,512]{1,0:T(8,128)(2,1)S(1)}, u32[]{:S(2)}, u32[]{:S(2)}) collective-permute-start(bf16[48,512]{1,0:T(8,128)(2,1)S(1)} %get-tuple-element.45), channel_id=1, source_target_pairs={{0,28},{4,24},{8,20},{12,16},{16,12},{20,8},{24,4},{28,0},{1,29},{... | collective-permute-start | bytes 147464 | tf_op jit(solution)/shard_map/ppermute | solution.py:43
  26.9 4.9 %collective-permute-start.10 = (bf16[48,512]{1,0:T(8,128)(2,1)S(1)}, bf16[48,512]{1,0:T(8,128)(2,1)S(1)}, u32[]{:S(2)}, u32[]{:S(2)}) collective-permute-start(bf16[48,512]{1,0:T(8,128)(2,1)S(1)} %get-tuple-element.53), channel_id=1, source_target_pairs={{0,4},{4,0},{8,12},{12,8},{16,20},{20,16},{24,28},{28,24},{1,5},{5... | collective-permute-start | bytes 147464 | tf_op jit(solution)/shard_map/ppermute | solution.py:43
  27.1 6.8 %collective-permute-start.11 = (bf16[48,512]{1,0:T(8,128)(2,1)S(1)}, bf16[48,512]{1,0:T(8,128)(2,1)S(1)}, u32[]{:S(2)}, u32[]{:S(2)}) collective-permute-start(bf16[48,512]{1,0:T(8,128)(2,1)S(1)} %get-tuple-element.54), channel_id=1, source_target_pairs={{0,8},{4,12},{8,0},{12,4},{16,24},{20,28},{24,16},{28,20},{1,9},{5... | collective-permute-start | bytes 147464 | tf_op jit(solution)/shard_map/ppermute | solution.py:43
  29.0 6.2 %collective-permute-start.12 = (bf16[48,512]{1,0:T(8,128)(2,1)S(1)}, bf16[48,512]{1,0:T(8,128)(2,1)S(1)}, u32[]{:S(2)}, u32[]{:S(2)}) collective-permute-start(bf16[48,512]{1,0:T(8,128)(2,1)S(1)} %get-tuple-element.55), channel_id=1, source_target_pairs={{0,12},{4,8},{8,4},{12,0},{16,28},{20,24},{24,20},{28,16},{1,13},{... | collective-permute-start | bytes 147464 | tf_op jit(solution)/shard_map/ppermute | solution.py:43
  29.0 6.2 %collective-permute-start.13 = (bf16[48,512]{1,0:T(8,128)(2,1)S(1)}, bf16[48,512]{1,0:T(8,128)(2,1)S(1)}, u32[]{:S(2)}, u32[]{:S(2)}) collective-permute-start(bf16[48,512]{1,0:T(8,128)(2,1)S(1)} %get-tuple-element.56), channel_id=1, source_target_pairs={{0,16},{4,20},{8,24},{12,28},{16,0},{20,4},{24,8},{28,12},{1,17},{... | collective-permute-start | bytes 147464 | tf_op jit(solution)/shard_map/ppermute | solution.py:43
  31.8 7.0 %collective-permute-start.14 = (bf16[48,512]{1,0:T(8,128)(2,1)S(1)}, bf16[48,512]{1,0:T(8,128)(2,1)S(1)}, u32[]{:S(2)}, u32[]{:S(2)}) collective-permute-start(bf16[48,512]{1,0:T(8,128)(2,1)S(1)} %get-tuple-element.57), channel_id=1, source_target_pairs={{0,20},{4,16},{8,28},{12,24},{16,4},{20,0},{24,12},{28,8},{1,21},{... | collective-permute-start | bytes 147464 | tf_op jit(solution)/shard_map/ppermute | solution.py:43
  31.8 7.0 %collective-permute-start.15 = (bf16[48,512]{1,0:T(8,128)(2,1)S(1)}, bf16[48,512]{1,0:T(8,128)(2,1)S(1)}, u32[]{:S(2)}, u32[]{:S(2)}) collective-permute-start(bf16[48,512]{1,0:T(8,128)(2,1)S(1)} %get-tuple-element.58), channel_id=1, source_target_pairs={{0,24},{4,28},{8,16},{12,20},{16,8},{20,12},{24,0},{28,4},{1,25},{... | collective-permute-start | bytes 147464 | tf_op jit(solution)/shard_map/ppermute | solution.py:43
  33.9 5.4 %collective-permute-start.16 = (bf16[48,512]{1,0:T(8,128)(2,1)S(1)}, bf16[48,512]{1,0:T(8,128)(2,1)S(1)}, u32[]{:S(2)}, u32[]{:S(2)}) collective-permute-start(bf16[48,512]{1,0:T(8,128)(2,1)S(1)} %get-tuple-element.59), channel_id=1, source_target_pairs={{0,28},{4,24},{8,20},{12,16},{16,12},{20,8},{24,4},{28,0},{1,29},{... | collective-permute-start | bytes 147464 | tf_op jit(solution)/shard_map/ppermute | solution.py:43
  39.6 4.0 %collective-permute-start.17 = (bf16[32,512]{1,0:T(8,128)(2,1)S(1)}, bf16[32,512]{1,0:T(8,128)(2,1)S(1)}, u32[]{:S(2)}, u32[]{:S(2)}) collective-permute-start(bf16[32,512]{1,0:T(8,128)(2,1)S(1)} %get-tuple-element.62), channel_id=1, source_target_pairs={{0,1},{1,0},{2,3},{3,2},{4,5},{5,4},{6,7},{7,6},{8,9},{9,8},{10,11... | collective-permute-start | bytes 98312 | tf_op jit(solution)/shard_map/ppermute | solution.py:43
  40.2 3.9 %collective-permute-start.18 = (bf16[32,512]{1,0:T(8,128)(2,1)S(1)}, bf16[32,512]{1,0:T(8,128)(2,1)S(1)}, u32[]{:S(2)}, u32[]{:S(2)}) collective-permute-start(bf16[32,512]{1,0:T(8,128)(2,1)S(1)} %get-tuple-element.63), channel_id=1, source_target_pairs={{0,2},{1,3},{2,0},{3,1},{4,6},{5,7},{6,4},{7,5},{8,10},{9,11},{10,... | collective-permute-start | bytes 98312 | tf_op jit(solution)/shard_map/ppermute | solution.py:43
  41.7 4.8 %collective-permute-start.19 = (bf16[32,512]{1,0:T(8,128)(2,1)S(1)}, bf16[32,512]{1,0:T(8,128)(2,1)S(1)}, u32[]{:S(2)}, u32[]{:S(2)}) collective-permute-start(bf16[32,512]{1,0:T(8,128)(2,1)S(1)} %get-tuple-element.64), channel_id=1, source_target_pairs={{0,3},{1,2},{2,1},{3,0},{4,7},{5,6},{6,5},{7,4},{8,11},{9,10},{10,... | collective-permute-start | bytes 98312 | tf_op jit(solution)/shard_map/ppermute | solution.py:43

commit v2 on v0

--- a/solution.py
+++ b/solution.py
@@ -11,6 +11,7 @@
 BF16, F32, I32 = jnp.bfloat16, jnp.float32, jnp.int32
 CHUNKS = 8
 LANES = 128
+PARTS = 4
 
 
 def iota(shape, dim):
@@ -36,10 +37,11 @@
 
 
 def swap(xs, axis):
-    n = len(xs)
-    out = [xs[0]]
-    for j in range(1, n):
-        out.append(lax.ppermute(xs[j], axis, [(i, partner(i, j, n)) for i in range(n)]))
+    n = lax.axis_size(axis)
+    out = []
+    for j, x in enumerate(xs):
+        pairs = [(i, partner(i, j, n)) for i in range(n)]
+        out.append(lax.ppermute(x, axis, pairs) if j else x)
     return out
 
 
@@ -122,26 +124,24 @@
         ref[...] = value[j * piece:(j + 1) * piece, :]
 
 
-def expert_kernel(steps, *refs):
-    ins, outs = refs[:steps], refs[steps + 4:2 * steps + 4]
-    gate_ref, up_ref, down_ref, order_ref = refs[steps:steps + 4]
-    x_ref, y_ref = refs[2 * steps + 4:]
-    total, lanes = y_ref.shape
-    piece = total // steps
-    count = total // CHUNKS
-    nt = ((1,), (1,))
+def expert_kernel(pieces, *refs):
+    ins, outs = refs[:pieces], refs[pieces + 4:2 * pieces + 4]
+    gate_ref, up_ref, down_ref, order_ref = refs[pieces:pieces + 4]
+    x_ref, rows_ref = refs[2 * pieces + 4:]
+    piece, lanes = ins[0].shape
+    count = x_ref.shape[0]
     for j, ref in enumerate(ins):
-        y_ref[j * piece:(j + 1) * piece, :] = ref[...]
-    x = mm(order_ref[...], y_ref[...]).astype(BF16)
+        rows_ref[j * piece:(j + 1) * piece, :] = ref[...]
+    x = mm(order_ref[...], rows_ref[...]).astype(BF16)
     for c in range(CHUNKS):
         x_ref[:, c * lanes:(c + 1) * lanes] = x[c * count:(c + 1) * count, :]
-    gate = mm(x_ref[...], gate_ref[...], nt)
-    up = mm(x_ref[...], up_ref[...], nt)
+    gate = mm(x_ref[...], gate_ref[...])
+    up = mm(x_ref[...], up_ref[...])
     hidden = (gate / (1.0 + jnp.exp(-gate)) * up).astype(BF16)
     for c in range(CHUNKS):
         value = mm(hidden, down_ref[:, c * lanes:(c + 1) * lanes]).astype(BF16)
-        y_ref[c * count:(c + 1) * count, :] = value
-    y = mm(order_ref[...], y_ref[...], ((0,), (0,))).astype(BF16)
+        rows_ref[c * count:(c + 1) * count, :] = value
+    y = mm(order_ref[...], rows_ref[...], ((0,), (0,))).astype(BF16)
     for j, ref in enumerate(outs):
         ref[...] = y[j * piece:(j + 1) * piece, :]
 
@@ -184,17 +184,43 @@
     return pltpu.with_memory_space_constraint(x, pltpu.HBM)
 
 
-def fetch_kernel(n_expert, topk, *refs):
-    ins, pick_ref, small_ref, outs, order_ref, mix_ref, sems = (
-        refs[:3], refs[3], refs[4], refs[5:8], refs[8], refs[9], refs[10]
-    )
-    copies = [pltpu.make_async_copy(a, b, sems.at[i]) for i, (a, b) in enumerate(zip(ins, outs))]
-    for copy in copies:
+def copies_of(source, target, sems, at):
+    part = source.shape[0] // PARTS
+    rows = [pl.ds(p * part, part) for p in range(PARTS)]
+    return [
+        pltpu.make_async_copy(source.at[r], target.at[r], sems.at[at + p]) for p, r in enumerate(rows)
+    ]
+
+
+def turn(source, target):
+    width = source.shape[1] // CHUNKS
+    for c in range(CHUNKS):
+        target[c * width:(c + 1) * width, :] = source[:, c * width:(c + 1) * width].T
+
+
+def fetch_kernel(gate_hbm, up_hbm, gate_ref, up_ref, order_ref, held, sems):
+    first = copies_of(gate_hbm, held, sems, 0)
+    second = copies_of(up_hbm, up_ref, sems, PARTS)
+    for copy in first + second:
         copy.start()
-    total, columns = pick_ref.shape
+    total = order_ref.shape[0]
     count = total // CHUNKS
     row, col = iota((total, total), 0), iota((total, total), 1)
     order_ref[...] = onehot(col == (row % count) * CHUNKS + row // count)
+    for copy in first:
+        copy.wait()
+    turn(held, gate_ref)
+    for copy in second:
+        copy.wait()
+
+
+def prepare_kernel(n_expert, topk, up_ref, down_hbm, pick_ref, small_ref, *refs):
+    turned_ref, down_ref, mix_ref, sems = refs
+    copies = copies_of(down_hbm, down_ref, sems, 0)
+    for copy in copies:
+        copy.start()
+    turn(up_ref, turned_ref)
+    total, columns = pick_ref.shape
     _, expert = row_experts(total, columns, total // n_expert, n_expert)
     gate = jnp.zeros((total, columns), F32)
     for k in range(topk):
@@ -210,7 +236,7 @@
     count, width = tokens.shape
     topk = expert_ids.shape[1]
     group = count * n_dp
-    assert group <= LANES and n_expert < 256 and width % (CHUNKS * LANES) == 0
+    assert group <= LANES and w_gate.shape[1] % (16 * PARTS) == 0 and n_expert < 256 and width % (CHUNKS * LANES) == 0
     assert width >= 2 * CHUNKS * LANES and placement.shape[1] <= 8
     first = max(2, group * topk // n_expert)
     slots = first + max(1, first // 2)
@@ -245,28 +271,34 @@
         scratch=(pltpu.VMEM((columns, lanes), BF16),),
         limit=48 << 20 if big else 8 << 20,
     )(*blocks, spread, earlier)
-    weights = [w[0] for w in (w_gate, w_up, w_down)]
     vmem = pl.BlockSpec(memory_space=pltpu.VMEM)
-    *weights, order, mix = call(
-        functools.partial(fetch_kernel, n_expert, topk),
-        [shape(*w.shape) for w in weights] + [shape(total, total), shape(total, columns)],
-        [hbm] * 3 + [vmem] * 2,
-        (pltpu.SemaphoreType.DMA((3,)),),
+    piece = slots * CHUNKS
+    block = w_gate.shape[1:]
+    turned = shape(*block[::-1])
+    gate, up, order = call(
+        fetch_kernel,
+        [turned, shape(*block), shape(total, total)],
+        [hbm] * 2,
+        (pltpu.VMEM(block, BF16), pltpu.SemaphoreType.DMA((2 * PARTS,))),
         limit=48 << 20 if big else 16 << 20,
-        cost_estimate=pl.CostEstimate(
-            flops=0, bytes_accessed=sum(4 * w.size for w in weights), transcendentals=0
-        ),
-    )(*map(in_hbm, weights), pick, small)
+    )(in_hbm(w_gate[0]), in_hbm(w_up[0]))
+    up, down, mix = call(
+        functools.partial(prepare_kernel, n_expert, topk),
+        [turned, shape(*block), shape(total, columns)],
+        [vmem, hbm, vmem, vmem],
+        (pltpu.SemaphoreType.DMA((PARTS,)),),
+        limit=48 << 20 if big else 16 << 20,
+    )(up, in_hbm(w_down[0]), pick, small)
     rows = swap(sends, "expert")
     parts = call(
         functools.partial(expert_kernel, n_expert),
-        [shape(slots * CHUNKS, lanes)] * n_expert,
+        [shape(piece, lanes)] * n_expert,
         scratch=(
             pltpu.VMEM((total // CHUNKS, width), BF16),
             pltpu.VMEM((total, lanes), BF16),
         ),
         limit=60 << 20 if big else 24 << 20,
-    )(*rows, *weights, order)
+    )(*rows, gate, up, down, order)
     backs = swap(parts, "expert")
     outs = call(
         functools.partial(mix_kernel, n_expert),

time: 47.3 us -> 47.5 us (level)
    pallas_call x2 -> x3, Pallas kernels: 6.64 us -> 6.87 us  [the longest x1 2.86 us: body(): call(fetch_kernel, [turned, shape(*block), shape(total, total)], [hbm] *...]
  transfers between devices with their start and end apart: 20 -> 20, of which waited for: 9 -> 9; matrix products, arithmetic and copies ran while one was open for 0% -> 0% of each run, Pallas kernels for 8% -> 10%
where the time goes in v2:
time: 47.5 us; the launch traced here: 47.3 us
  starting transfers between devices  24.7 us (52%)
  waiting for transfers between devices  13.1 us (28%)
  Pallas kernels  9.37 us (20%)
    ppermute x20, starting transfers between devices, swap(): out.append(lax.ppermute(x, axis, pairs) if j else x)  24.7 us
    ppermute x20, waiting for transfers between devices, swap(): out.append(lax.ppermute(x, axis, pairs) if j else x)  13.1 us
    pallas_call x1, Pallas kernels, body(): call(fetch_kernel, [turned, shape(*block), shape(total, total)], [hbm] *...  2.86 us
    pallas_call x1, Pallas kernels, body(): call(functools.partial(expert_kernel, n_expert), [shape(piece, lanes)] *...  2.13 us
    pallas_call x1, Pallas kernels, body(): call(functools.partial(prepare_kernel, n_expert, topk), [turned, shape(*b...  1.88 us
    pallas_call x1, Pallas kernels, body(): call(pack_kernel, [shape(per + extra, lanes), table, table], [hbm] * 4, (...  1.08 us
  transfers between devices with their start and end apart: 20, of which 9 were waited for; matrix products, arithmetic and copies ran while one was open for 0% of the time, Pallas kernels for 10%

profile of v2, /device:TPU:0, one launch (start us, length us, event | category | flops | bytes accessed | tf_op | source)
XLA Modules:
  0.0 47.3 jit_solution(26139729373297790)
XLA Ops:
  0.0 1.1 %shard_map.73 = (bf16[40,512]{1,0:T(8,128)(2,1)S(1)}, bf16[128,128]{1,0:T(8,128)(2,1)S(1)}, bf16[128,128]{1,0:T(8,128)(2,1)S(1)}) custom-call(bf16[4,4096]{1,0:T(4,128)(2,1)} %tok_hbm.1, s32[2,4]{1,0:T(2,128)} %bitcast.8, bf16[2,4]{1,0:T(2,128)(2,1)} %bitcast.9, s32[2,2]{1,0:T(2,128)} %place_hbm.1), custom_call_target="tpu_custom_call" | custom-call | tf_op jit(solution)/shard_map/pallas_call | solution.py:253
  1.1 4.0 %collective-permute-start.2 = (bf16[40,512]{1,0:T(8,128)(2,1)S(1)}, bf16[40,512]{1,0:T(8,128)(2,1)S(1)}, u32[]{:S(2)}, u32[]{:S(2)}) collective-permute-start(bf16[40,512]{1,0:T(8,128)(2,1)S(1)} %get-tuple-element.36.refs_0_), channel_id=1, source_target_pairs={{0,3},{1,2},{2,1},{3,0},{4,7},{5,6},{6,5},{7,4},{8,11},{9,10},{10,... | collective-permute-start | bytes 122888 | tf_op jit(solution)/shard_map/ppermute | solution.py:44
  5.1 0.5 %collective-permute-start.1 = (bf16[40,512]{1,0:T(8,128)(2,1)S(1)}, bf16[40,512]{1,0:T(8,128)(2,1)S(1)}, u32[]{:S(2)}, u32[]{:S(2)}) collective-permute-start(bf16[40,512]{1,0:T(8,128)(2,1)S(1)} %get-tuple-element.36.refs_0_), channel_id=1, source_target_pairs={{0,2},{1,3},{2,0},{3,1},{4,6},{5,7},{6,4},{7,5},{8,10},{9,11},{10,... | collective-permute-start | bytes 122888 | tf_op jit(solution)/shard_map/ppermute | solution.py:44
  5.6 0.1 collective-permute-start
  5.7 1.3 %collective-permute-done.2.refs_3_ = bf16[40,512]{1,0:T(8,128)(2,1)S(1)} collective-permute-done((bf16[40,512]{1,0:T(8,128)(2,1)S(1)}, bf16[40,512]{1,0:T(8,128)(2,1)S(1)}, u32[]{:S(2)}, u32[]{:S(2)}) %collective-permute-start.2) | collective-permute-done | bytes 40992 | tf_op jit(solution)/shard_map/ppermute | solution.py:44
  7.1 2.0 %collective-permute-done.1.refs_2_ = bf16[40,512]{1,0:T(8,128)(2,1)S(1)} collective-permute-done((bf16[40,512]{1,0:T(8,128)(2,1)S(1)}, bf16[40,512]{1,0:T(8,128)(2,1)S(1)}, u32[]{:S(2)}, u32[]{:S(2)}) %collective-permute-start.1) | collective-permute-done | bytes 40992 | tf_op jit(solution)/shard_map/ppermute | solution.py:44
  9.1 0.5 %collective-permute-done.refs_1_ = bf16[40,512]{1,0:T(8,128)(2,1)S(1)} collective-permute-done((bf16[40,512]{1,0:T(8,128)(2,1)S(1)}, bf16[40,512]{1,0:T(8,128)(2,1)S(1)}, u32[]{:S(2)}, u32[]{:S(2)}) %collective-permute-start) | collective-permute-done | bytes 40992 | tf_op jit(solution)/shard_map/ppermute | solution.py:44
  9.6 0.5 %shard_map.74 = (bf16[48,512]{1,0:T(8,128)(2,1)S(1)}, bf16[48,512]{1,0:T(8,128)(2,1)S(1)}, bf16[48,512]{1,0:T(8,128)(2,1)S(1)}, bf16[48,512]{1,0:T(8,128)(2,1)S(...) custom-call(bf16[40,512]{1,0:T(8,128)(2,1)S(1)} %get-tuple-element.3, ...), custom_call_target="tpu_custom_call" | custom-call | tf_op jit(solution)/shard_map/pallas_call | solution.py:267
  10.2 1.6 %collective-permute-start.4 = (bf16[48,512]{1,0:T(8,128)(2,1)S(1)}, bf16[48,512]{1,0:T(8,128)(2,1)S(1)}, u32[]{:S(2)}, u32[]{:S(2)}) collective-permute-start(bf16[48,512]{1,0:T(8,128)(2,1)S(1)} %get-tuple-element.41), channel_id=1, source_target_pairs={{0,8},{4,12},{8,0},{12,4},{16,24},{20,28},{24,16},{28,20},{1,9},{5... | collective-permute-start | bytes 147464 | tf_op jit(solution)/shard_map/ppermute | solution.py:44
  11.9 0.2 collective-permute-start.5
  12.1 2.6 %collective-permute-start.6 = (bf16[48,512]{1,0:T(8,128)(2,1)S(1)}, bf16[48,512]{1,0:T(8,128)(2,1)S(1)}, u32[]{:S(2)}, u32[]{:S(2)}) collective-permute-start(bf16[48,512]{1,0:T(8,128)(2,1)S(1)} %get-tuple-element.43), channel_id=1, source_target_pairs={{0,16},{4,20},{8,24},{12,28},{16,0},{20,4},{24,8},{28,12},{1,17},{... | collective-permute-start | bytes 147464 | tf_op jit(solution)/shard_map/ppermute | solution.py:44
  14.7 3.6 %collective-permute-start.8 = (bf16[48,512]{1,0:T(8,128)(2,1)S(1)}, bf16[48,512]{1,0:T(8,128)(2,1)S(1)}, u32[]{:S(2)}, u32[]{:S(2)}) collective-permute-start(bf16[48,512]{1,0:T(8,128)(2,1)S(1)} %get-tuple-element.45), channel_id=1, source_target_pairs={{0,24},{4,28},{8,16},{12,20},{16,8},{20,12},{24,0},{28,4},{1,25},{... | collective-permute-start | bytes 147464 | tf_op jit(solution)/shard_map/ppermute | solution.py:44
  18.3 0.1 collective-permute-start.9
  18.4 2.9 %shard_map.75 = (bf16[4096,384]{1,0:T(8,128)(2,1)S(1)}, bf16[384,4096]{1,0:T(8,128)(2,1)S(1)}, bf16[384,384]{1,0:T(8,128)(2,1)S(1)}) custom-call(bf16[384,4096]{1,0:T(8,128)(2,1)} %bitcast.5, bf16[384,4096]{1,0:T(8,128)(2,1)} %bitcast.6), custom_call_target="tpu_custom_call" | custom-call | tf_op jit(solution)/shard_map/pallas_call | solution.py:278
  21.3 1.9 %shard_map.76 = (bf16[4096,384]{1,0:T(8,128)(2,1)S(1)}, bf16[384,4096]{1,0:T(8,128)(2,1)S(1)}, bf16[384,128]{1,0:T(8,128)(2,1)S(1)}) custom-call(bf16[384,4096]{1,0:T(8,128)(2,1)S(1)} %get-tuple-element.48.up_ref, bf16[384,4096]{1,0:T(8,128)(2,1)} %bitcast.7, bf16[384,128]{1,0:T(8,128)(2,1)S(1)} %get-tuple-element.49.pick_ref, ...), custom_call_target="tpu_custom_call" | custom-call | tf_op jit(solution)/shard_map/pallas_call | solution.py:285
  23.2 0.7 %collective-permute-done.9.refs_7_ = bf16[48,512]{1,0:T(8,128)(2,1)S(1)} collective-permute-done((bf16[48,512]{1,0:T(8,128)(2,1)S(1)}, bf16[48,512]{1,0:T(8,128)(2,1)S(1)}, u32[]{:S(2)}, u32[]{:S(2)}) %collective-permute-start.9) | collective-permute-done | bytes 49184 | tf_op jit(solution)/shard_map/ppermute | solution.py:44
  23.9 2.1 %shard_map.77 = (bf16[48,512]{1,0:T(8,128)(2,1)S(1)}, bf16[48,512]{1,0:T(8,128)(2,1)S(1)}, bf16[48,512]{1,0:T(8,128)(2,1)S(1)}, bf16[48,512]{1,0:T(8,128)(2,1)S(...) custom-call(bf16[48,512]{1,0:T(8,128)(2,1)S(1)} %get-tuple-element.3, ...), custom_call_target="tpu_custom_call" | custom-call | tf_op jit(solution)/shard_map/pallas_call | solution.py:293
  26.0 0.2 collective-permute-start.10
  26.2 1.9 %collective-permute-start.11 = (bf16[48,512]{1,0:T(8,128)(2,1)S(1)}, bf16[48,512]{1,0:T(8,128)(2,1)S(1)}, u32[]{:S(2)}, u32[]{:S(2)}) collective-permute-start(bf16[48,512]{1,0:T(8,128)(2,1)S(1)} %get-tuple-element.56), channel_id=1, source_target_pairs={{0,8},{4,12},{8,0},{12,4},{16,24},{20,28},{24,16},{28,20},{1,9},{5... | collective-permute-start | bytes 147464 | tf_op jit(solution)/shard_map/ppermute | solution.py:44
  28.1 2.8 %collective-permute-start.13 = (bf16[48,512]{1,0:T(8,128)(2,1)S(1)}, bf16[48,512]{1,0:T(8,128)(2,1)S(1)}, u32[]{:S(2)}, u32[]{:S(2)}) collective-permute-start(bf16[48,512]{1,0:T(8,128)(2,1)S(1)} %get-tuple-element.58), channel_id=1, source_target_pairs={{0,16},{4,20},{8,24},{12,28},{16,0},{20,4},{24,8},{28,12},{1,17},{... | collective-permute-start | bytes 147464 | tf_op jit(solution)/shard_map/ppermute | solution.py:44
  30.9 2.7 %collective-permute-start.15 = (bf16[48,512]{1,0:T(8,128)(2,1)S(1)}, bf16[48,512]{1,0:T(8,128)(2,1)S(1)}, u32[]{:S(2)}, u32[]{:S(2)}) collective-permute-start(bf16[48,512]{1,0:T(8,128)(2,1)S(1)} %get-tuple-element.60), channel_id=1, source_target_pairs={{0,24},{4,28},{8,16},{12,20},{16,8},{20,12},{24,0},{28,4},{1,25},{... | collective-permute-start | bytes 147464 | tf_op jit(solution)/shard_map/ppermute | solution.py:44
  33.6 0.7 %collective-permute-start.16 = (bf16[48,512]{1,0:T(8,128)(2,1)S(1)}, bf16[48,512]{1,0:T(8,128)(2,1)S(1)}, u32[]{:S(2)}, u32[]{:S(2)}) collective-permute-start(bf16[48,512]{1,0:T(8,128)(2,1)S(1)} %get-tuple-element.61), channel_id=1, source_target_pairs={{0,28},{4,24},{8,20},{12,16},{16,12},{20,8},{24,4},{28,0},{1,29},{... | collective-permute-start | bytes 147464 | tf_op jit(solution)/shard_map/ppermute | solution.py:44
  34.4 3.6 %collective-permute-done.14.refs_5_ = bf16[48,512]{1,0:T(8,128)(2,1)S(1)} collective-permute-done((bf16[48,512]{1,0:T(8,128)(2,1)S(1)}, bf16[48,512]{1,0:T(8,128)(2,1)S(1)}, u32[]{:S(2)}, u32[]{:S(2)}) %collective-permute-start.14) | collective-permute-done | bytes 49184 | tf_op jit(solution)/shard_map/ppermute | solution.py:44
  37.9 1.6 %collective-permute-done.16.refs_7_ = bf16[48,512]{1,0:T(8,128)(2,1)S(1)} collective-permute-done((bf16[48,512]{1,0:T(8,128)(2,1)S(1)}, bf16[48,512]{1,0:T(8,128)(2,1)S(1)}, u32[]{:S(2)}, u32[]{:S(2)}) %collective-permute-start.16) | collective-permute-done | bytes 49184 | tf_op jit(solution)/shard_map/ppermute | solution.py:44
  39.5 0.2 shard_map.78
  39.8 0.6 %collective-permute-start.17 = (bf16[32,512]{1,0:T(8,128)(2,1)S(1)}, bf16[32,512]{1,0:T(8,128)(2,1)S(1)}, u32[]{:S(2)}, u32[]{:S(2)}) collective-permute-start(bf16[32,512]{1,0:T(8,128)(2,1)S(1)} %get-tuple-element.64), channel_id=1, source_target_pairs={{0,1},{1,0},{2,3},{3,2},{4,5},{5,4},{6,7},{7,6},{8,9},{9,8},{10,11... | collective-permute-start | bytes 98312 | tf_op jit(solution)/shard_map/ppermute | solution.py:44
  40.4 1.5 %collective-permute-start.18 = (bf16[32,512]{1,0:T(8,128)(2,1)S(1)}, bf16[32,512]{1,0:T(8,128)(2,1)S(1)}, u32[]{:S(2)}, u32[]{:S(2)}) collective-permute-start(bf16[32,512]{1,0:T(8,128)(2,1)S(1)} %get-tuple-element.65), channel_id=1, source_target_pairs={{0,2},{1,3},{2,0},{3,1},{4,6},{5,7},{6,4},{7,5},{8,10},{9,11},{10,... | collective-permute-start | bytes 98312 | tf_op jit(solution)/shard_map/ppermute | solution.py:44
  41.9 1.4 %collective-permute-start.19 = (bf16[32,512]{1,0:T(8,128)(2,1)S(1)}, bf16[32,512]{1,0:T(8,128)(2,1)S(1)}, u32[]{:S(2)}, u32[]{:S(2)}) collective-permute-start(bf16[32,512]{1,0:T(8,128)(2,1)S(1)} %get-tuple-element.66), channel_id=1, source_target_pairs={{0,3},{1,2},{2,1},{3,0},{4,7},{5,6},{6,5},{7,4},{8,11},{9,10},{10,... | collective-permute-start | bytes 98312 | tf_op jit(solution)/shard_map/ppermute | solution.py:44
  43.3 0.4 collective-permute-done.17.refs_1_
  43.7 0.5 %collective-permute-done.18.refs_2_ = bf16[32,512]{1,0:T(8,128)(2,1)S(1)} collective-permute-done((bf16[32,512]{1,0:T(8,128)(2,1)S(1)}, bf16[32,512]{1,0:T(8,128)(2,1)S(1)}, u32[]{:S(2)}, u32[]{:S(2)}) %collective-permute-start.18) | collective-permute-done | bytes 32800 | tf_op jit(solution)/shard_map/ppermute | solution.py:44
  44.3 2.4 %collective-permute-done.19.refs_3_ = bf16[32,512]{1,0:T(8,128)(2,1)S(1)} collective-permute-done((bf16[32,512]{1,0:T(8,128)(2,1)S(1)}, bf16[32,512]{1,0:T(8,128)(2,1)S(1)}, u32[]{:S(2)}, u32[]{:S(2)}) %collective-permute-start.19) | collective-permute-done | bytes 32800 | tf_op jit(solution)/shard_map/ppermute | solution.py:44
  46.7 0.6 %shard_map.79 = bf16[4,4096]{1,0:T(4,128)(2,1)} custom-call(bf16[32,512]{1,0:T(8,128)(2,1)S(1)} %get-tuple-element.63.refs_0_, bf16[32,512]{1,0:T(8,128)(2,1)S(1)} %collective-permute-done.17.refs_1_, bf16[32,512]{1,0:T(8,128)(2,1)S(1)} %collective-permute-done.18.refs_2_, bf16[32,512]{1,0:T(8,128)(2,1)S(1)} %collective-permute-done.19.refs_3_), custom_call_target="tpu_custom_call" | custom-call | tf_op jit(solution)/shard_map/pallas_call | solution.py:310
  (15 shorter events, 0.1 us)
Async XLA Ops:
  1.1 6.0 %collective-permute-start.2 = (bf16[40,512]{1,0:T(8,128)(2,1)S(1)}, bf16[40,512]{1,0:T(8,128)(2,1)S(1)}, u32[]{:S(2)}, u32[]{:S(2)}) collective-permute-start(bf16[40,512]{1,0:T(8,128)(2,1)S(1)} %get-tuple-element.36.refs_0_), channel_id=1, source_target_pairs={{0,3},{1,2},{2,1},{3,0},{4,7},{5,6},{6,5},{7,4},{8,11},{9,10},{10,... | collective-permute-start | bytes 122888 | tf_op jit(solution)/shard_map/ppermute | solution.py:44
  5.1 4.0 %collective-permute-start.1 = (bf16[40,512]{1,0:T(8,128)(2,1)S(1)}, bf16[40,512]{1,0:T(8,128)(2,1)S(1)}, u32[]{:S(2)}, u32[]{:S(2)}) collective-permute-start(bf16[40,512]{1,0:T(8,128)(2,1)S(1)} %get-tuple-element.36.refs_0_), channel_id=1, source_target_pairs={{0,2},{1,3},{2,0},{3,1},{4,6},{5,7},{6,4},{7,5},{8,10},{9,11},{10,... | collective-permute-start | bytes 122888 | tf_op jit(solution)/shard_map/ppermute | solution.py:44
  5.6 4.0 %collective-permute-start = (bf16[40,512]{1,0:T(8,128)(2,1)S(1)}, bf16[40,512]{1,0:T(8,128)(2,1)S(1)}, u32[]{:S(2)}, u32[]{:S(2)}) collective-permute-start(bf16[40,512]{1,0:T(8,128)(2,1)S(1)} %get-tuple-element.36.refs_0_), channel_id=1, source_target_pairs={{0,1},{1,0},{2,3},{3,2},{4,5},{5,4},{6,7},{7,6},{8,9},{9,8},{10,11... | collective-permute-start | bytes 122888 | tf_op jit(solution)/shard_map/ppermute | solution.py:44
  10.1 4.5 %collective-permute-start.3 = (bf16[48,512]{1,0:T(8,128)(2,1)S(1)}, bf16[48,512]{1,0:T(8,128)(2,1)S(1)}, u32[]{:S(2)}, u32[]{:S(2)}) collective-permute-start(bf16[48,512]{1,0:T(8,128)(2,1)S(1)} %get-tuple-element.40), channel_id=1, source_target_pairs={{0,4},{4,0},{8,12},{12,8},{16,20},{20,16},{24,28},{28,24},{1,5},{5... | collective-permute-start | bytes 147464 | tf_op jit(solution)/shard_map/ppermute | solution.py:44
  10.2 8.1 %collective-permute-start.4 = (bf16[48,512]{1,0:T(8,128)(2,1)S(1)}, bf16[48,512]{1,0:T(8,128)(2,1)S(1)}, u32[]{:S(2)}, u32[]{:S(2)}) collective-permute-start(bf16[48,512]{1,0:T(8,128)(2,1)S(1)} %get-tuple-element.41), channel_id=1, source_target_pairs={{0,8},{4,12},{8,0},{12,4},{16,24},{20,28},{24,16},{28,20},{1,9},{5... | collective-permute-start | bytes 147464 | tf_op jit(solution)/shard_map/ppermute | solution.py:44
  11.9 11.3 %collective-permute-start.5 = (bf16[48,512]{1,0:T(8,128)(2,1)S(1)}, bf16[48,512]{1,0:T(8,128)(2,1)S(1)}, u32[]{:S(2)}, u32[]{:S(2)}) collective-permute-start(bf16[48,512]{1,0:T(8,128)(2,1)S(1)} %get-tuple-element.42), channel_id=1, source_target_pairs={{0,12},{4,8},{8,4},{12,0},{16,28},{20,24},{24,20},{28,16},{1,13},{... | collective-permute-start | bytes 147464 | tf_op jit(solution)/shard_map/ppermute | solution.py:44
  12.1 11.1 %collective-permute-start.6 = (bf16[48,512]{1,0:T(8,128)(2,1)S(1)}, bf16[48,512]{1,0:T(8,128)(2,1)S(1)}, u32[]{:S(2)}, u32[]{:S(2)}) collective-permute-start(bf16[48,512]{1,0:T(8,128)(2,1)S(1)} %get-tuple-element.43), channel_id=1, source_target_pairs={{0,16},{4,20},{8,24},{12,28},{16,0},{20,4},{24,8},{28,12},{1,17},{... | collective-permute-start | bytes 147464 | tf_op jit(solution)/shard_map/ppermute | solution.py:44
  14.6 8.5 %collective-permute-start.7 = (bf16[48,512]{1,0:T(8,128)(2,1)S(1)}, bf16[48,512]{1,0:T(8,128)(2,1)S(1)}, u32[]{:S(2)}, u32[]{:S(2)}) collective-permute-start(bf16[48,512]{1,0:T(8,128)(2,1)S(1)} %get-tuple-element.44), channel_id=1, source_target_pairs={{0,20},{4,16},{8,28},{12,24},{16,4},{20,0},{24,12},{28,8},{1,21},{... | collective-permute-start | bytes 147464 | tf_op jit(solution)/shard_map/ppermute | solution.py:44
  14.7 8.5 %collective-permute-start.8 = (bf16[48,512]{1,0:T(8,128)(2,1)S(1)}, bf16[48,512]{1,0:T(8,128)(2,1)S(1)}, u32[]{:S(2)}, u32[]{:S(2)}) collective-permute-start(bf16[48,512]{1,0:T(8,128)(2,1)S(1)} %get-tuple-element.45), channel_id=1, source_target_pairs={{0,24},{4,28},{8,16},{12,20},{16,8},{20,12},{24,0},{28,4},{1,25},{... | collective-permute-start | bytes 147464 | tf_op jit(solution)/shard_map/ppermute | solution.py:44
  18.3 5.6 %collective-permute-start.9 = (bf16[48,512]{1,0:T(8,128)(2,1)S(1)}, bf16[48,512]{1,0:T(8,128)(2,1)S(1)}, u32[]{:S(2)}, u32[]{:S(2)}) collective-permute-start(bf16[48,512]{1,0:T(8,128)(2,1)S(1)} %get-tuple-element.46), channel_id=1, source_target_pairs={{0,28},{4,24},{8,20},{12,16},{16,12},{20,8},{24,4},{28,0},{1,29},{... | collective-permute-start | bytes 147464 | tf_op jit(solution)/shard_map/ppermute | solution.py:44
  26.0 4.9 %collective-permute-start.10 = (bf16[48,512]{1,0:T(8,128)(2,1)S(1)}, bf16[48,512]{1,0:T(8,128)(2,1)S(1)}, u32[]{:S(2)}, u32[]{:S(2)}) collective-permute-start(bf16[48,512]{1,0:T(8,128)(2,1)S(1)} %get-tuple-element.55), channel_id=1, source_target_pairs={{0,4},{4,0},{8,12},{12,8},{16,20},{20,16},{24,28},{28,24},{1,5},{5... | collective-permute-start | bytes 147464 | tf_op jit(solution)/shard_map/ppermute | solution.py:44
  26.2 7.4 %collective-permute-start.11 = (bf16[48,512]{1,0:T(8,128)(2,1)S(1)}, bf16[48,512]{1,0:T(8,128)(2,1)S(1)}, u32[]{:S(2)}, u32[]{:S(2)}) collective-permute-start(bf16[48,512]{1,0:T(8,128)(2,1)S(1)} %get-tuple-element.56), channel_id=1, source_target_pairs={{0,8},{4,12},{8,0},{12,4},{16,24},{20,28},{24,16},{28,20},{1,9},{5... | collective-permute-start | bytes 147464 | tf_op jit(solution)/shard_map/ppermute | solution.py:44
  28.1 6.2 %collective-permute-start.12 = (bf16[48,512]{1,0:T(8,128)(2,1)S(1)}, bf16[48,512]{1,0:T(8,128)(2,1)S(1)}, u32[]{:S(2)}, u32[]{:S(2)}) collective-permute-start(bf16[48,512]{1,0:T(8,128)(2,1)S(1)} %get-tuple-element.57), channel_id=1, source_target_pairs={{0,12},{4,8},{8,4},{12,0},{16,28},{20,24},{24,20},{28,16},{1,13},{... | collective-permute-start | bytes 147464 | tf_op jit(solution)/shard_map/ppermute | solution.py:44
  28.1 6.2 %collective-permute-start.13 = (bf16[48,512]{1,0:T(8,128)(2,1)S(1)}, bf16[48,512]{1,0:T(8,128)(2,1)S(1)}, u32[]{:S(2)}, u32[]{:S(2)}) collective-permute-start(bf16[48,512]{1,0:T(8,128)(2,1)S(1)} %get-tuple-element.58), channel_id=1, source_target_pairs={{0,16},{4,20},{8,24},{12,28},{16,0},{20,4},{24,8},{28,12},{1,17},{... | collective-permute-start | bytes 147464 | tf_op jit(solution)/shard_map/ppermute | solution.py:44
  30.9 7.0 %collective-permute-start.14 = (bf16[48,512]{1,0:T(8,128)(2,1)S(1)}, bf16[48,512]{1,0:T(8,128)(2,1)S(1)}, u32[]{:S(2)}, u32[]{:S(2)}) collective-permute-start(bf16[48,512]{1,0:T(8,128)(2,1)S(1)} %get-tuple-element.59), channel_id=1, source_target_pairs={{0,20},{4,16},{8,28},{12,24},{16,4},{20,0},{24,12},{28,8},{1,21},{... | collective-permute-start | bytes 147464 | tf_op jit(solution)/shard_map/ppermute | solution.py:44
  30.9 7.0 %collective-permute-start.15 = (bf16[48,512]{1,0:T(8,128)(2,1)S(1)}, bf16[48,512]{1,0:T(8,128)(2,1)S(1)}, u32[]{:S(2)}, u32[]{:S(2)}) collective-permute-start(bf16[48,512]{1,0:T(8,128)(2,1)S(1)} %get-tuple-element.60), channel_id=1, source_target_pairs={{0,24},{4,28},{8,16},{12,20},{16,8},{20,12},{24,0},{28,4},{1,25},{... | collective-permute-start | bytes 147464 | tf_op jit(solution)/shard_map/ppermute | solution.py:44
  33.6 5.9 %collective-permute-start.16 = (bf16[48,512]{1,0:T(8,128)(2,1)S(1)}, bf16[48,512]{1,0:T(8,128)(2,1)S(1)}, u32[]{:S(2)}, u32[]{:S(2)}) collective-permute-start(bf16[48,512]{1,0:T(8,128)(2,1)S(1)} %get-tuple-element.61), channel_id=1, source_target_pairs={{0,28},{4,24},{8,20},{12,16},{16,12},{20,8},{24,4},{28,0},{1,29},{... | collective-permute-start | bytes 147464 | tf_op jit(solution)/shard_map/ppermute | solution.py:44
  39.8 4.0 %collective-permute-start.17 = (bf16[32,512]{1,0:T(8,128)(2,1)S(1)}, bf16[32,512]{1,0:T(8,128)(2,1)S(1)}, u32[]{:S(2)}, u32[]{:S(2)}) collective-permute-start(bf16[32,512]{1,0:T(8,128)(2,1)S(1)} %get-tuple-element.64), channel_id=1, source_target_pairs={{0,1},{1,0},{2,3},{3,2},{4,5},{5,4},{6,7},{7,6},{8,9},{9,8},{10,11... | collective-permute-start | bytes 98312 | tf_op jit(solution)/shard_map/ppermute | solution.py:44
  40.4 3.9 %collective-permute-start.18 = (bf16[32,512]{1,0:T(8,128)(2,1)S(1)}, bf16[32,512]{1,0:T(8,128)(2,1)S(1)}, u32[]{:S(2)}, u32[]{:S(2)}) collective-permute-start(bf16[32,512]{1,0:T(8,128)(2,1)S(1)} %get-tuple-element.65), channel_id=1, source_target_pairs={{0,2},{1,3},{2,0},{3,1},{4,6},{5,7},{6,4},{7,5},{8,10},{9,11},{10,... | collective-permute-start | bytes 98312 | tf_op jit(solution)/shard_map/ppermute | solution.py:44
  41.9 4.8 %collective-permute-start.19 = (bf16[32,512]{1,0:T(8,128)(2,1)S(1)}, bf16[32,512]{1,0:T(8,128)(2,1)S(1)}, u32[]{:S(2)}, u32[]{:S(2)}) collective-permute-start(bf16[32,512]{1,0:T(8,128)(2,1)S(1)} %get-tuple-element.66), channel_id=1, source_target_pairs={{0,3},{1,2},{2,1},{3,0},{4,7},{5,6},{6,5},{7,4},{8,11},{9,10},{10,... | collective-permute-start | bytes 98312 | tf_op jit(solution)/shard_map/ppermute | solution.py:44
